TPU v7x, 32 devices: a whole 2x2x4 slice. The times are simulated.
32 devices in a mesh: rollout: 2 (over y), branch: 4 (over z), seq: 4 (over x, core).
Axes of the slice: x: 2, y: 2, z: 4, core: 2. Of those that a mesh axis runs over, the one named last changes fastest.
Arguments:
- queries: bfloat16 [8, 512, 4096], P(('rollout', 'branch'), 'seq'), parts along dimension 0, may hold values from -8 to 8
- keyvals: bfloat16 [8, 512, 2, 256], P(('rollout', 'branch'), 'seq'), parts along dimension 0, may hold values from -4 to 4
- residual: bfloat16 [8, 512, 4096], P(('rollout', 'branch'), 'seq'), parts along dimension 0, may hold values from -3 to 3
- read_list: int32 [8, 4, 3], P(('rollout', 'branch'), 'seq'), parts along dimension 0, may hold values from 0 to 3
- router: bfloat16 [4096, 8], replicated, may hold values from -0.09375 to 0.09375
- expert_ids: int32 [8, 512, 2], P(('rollout', 'branch'), 'seq'), parts along dimension 0, may hold values from 0 to 7, all different within a row; in each aligned block of 128 rows (0 to 127, 128 to 255, ..., all dimensions but the last counted through in order) at most 48 rows name the same one
- w_gate_up: bfloat16 [16, 4096, 2, 384], P(('branch', 'seq')), may hold values from -0.09375 to 0.09375
- w_down: bfloat16 [16, 384, 4096], P(('branch', 'seq')), may hold values from -0.21875 to 0.21875
Outputs:
- mixed: bfloat16 [8, 512, 4096], P(('rollout', 'branch'), 'seq'), parts along dimension 0
There are 2 independent parts, one for each index of `rollout`. A program takes and returns all parts, laid end to end along the dimension named above; an argument that names none is the same for every part. Nothing has to cross between parts.
Inputs may be any that keep to these rules, and one draw needn't show every extreme that they name: read_list[c, s, o] is the block of branch c that query block s of branch (c + o + 1) mod 4 reads. `expert_ids`: each token names 2 different experts; of the 128 tokens of one device at most 48 name one expert, and in every draw some expert is named by exactly 48 tokens of some device.
All inputs are finite; a program needn't handle non-finite values.
Results may differ from a plain program's by a relative error of at most 0.0062.
Values may be sent and summed in bfloat16 or wider, within the bound.
A program may use at most 192 MiB of HBM per device.

v0:
```python
import functools
import math

import jax
import jax.numpy as jnp
from jax import lax
from jax.experimental import pallas as pl
from jax.experimental.pallas import tpu as pltpu
from jax.sharding import PartitionSpec as P

HEAD_SIZE = 128
PARTS = 4
VMEM_LIMIT = 60 * 1024 * 1024
F32 = jnp.float32
BF16 = jnp.bfloat16
ANY = pl.BlockSpec(memory_space=pl.ANY)
VMEM = pl.BlockSpec(memory_space=pltpu.VMEM)
SMEM = pl.BlockSpec(memory_space=pltpu.SMEM)


def flipped(number, mask, count):
    value, bit = 0, 1
    while bit < count:
        value = value + ((number // bit + mask // bit) % 2) * bit
        bit *= 2
    return value


def attend_kernel(
    experts, cap, n_branch, n_seq,
    list_ref, q_ref, own_ref, res_ref, router_ref, ids_ref, idt_ref,
    send_ref, state_ref, gate_ref, norm_ref, meta_ref,
    picked, sib_ref, tops, totals, ssem, rsem,
):
    branch = lax.axis_index("branch")
    seq = lax.axis_index("seq")
    me = (branch * n_seq + seq) // 2
    rows, width = q_ref.shape
    kv_heads = own_ref.shape[2] // (2 * HEAD_SIZE)
    group = width // HEAD_SIZE // kv_heads
    together = 2
    tall = together * rows
    own_len = n_seq * rows
    sib_len = (n_branch - 1) * rows
    scale = 1.0 / math.sqrt(HEAD_SIZE)
    nt = (((1,), (1,)), ((), ()))

    barrier = pltpu.get_barrier_semaphore()
    for step in range(1, n_branch):
        pl.semaphore_signal(
            barrier, inc=1, device_id={"branch": (branch + step) % n_branch},
            device_id_type=pl.DeviceIdType.MESH,
        )
    for offset in range(n_branch - 1):
        picked[offset] = own_ref[(seq - list_ref[offset] + n_seq) % n_seq]
    pl.semaphore_wait(barrier, n_branch - 1)
    copies = []
    for offset in range(n_branch - 1):
        copy = pltpu.make_async_remote_copy(
            src_ref=picked.at[offset], dst_ref=sib_ref.at[offset],
            send_sem=ssem.at[offset], recv_sem=rsem.at[offset],
            device_id={"branch": (branch + offset + 1) % n_branch},
            device_id_type=pl.DeviceIdType.MESH,
        )
        copy.start()
        copies.append(copy)

    at_row = lax.broadcasted_iota(jnp.int32, (tall, own_len), 0) % rows
    at_col = lax.broadcasted_iota(jnp.int32, (tall, own_len), 1)
    earlier = at_col // rows
    bias = jnp.where(
        earlier == 0,
        jnp.where(at_col <= at_row, 0.0, -1e30),
        jnp.where(earlier <= seq, 0.0, -1e30),
    )

    def head_parts(head, step):
        base = (head * group + step * together) * HEAD_SIZE
        cols = [
            pl.ds(pl.multiple_of(base + i * HEAD_SIZE, HEAD_SIZE), HEAD_SIZE)
            for i in range(together)
        ]
        return cols, jnp.concatenate([q_ref[:, c] for c in cols], axis=0)

    def kv_cols(head):
        return (
            slice(head * HEAD_SIZE, (head + 1) * HEAD_SIZE),
            slice((kv_heads + head) * HEAD_SIZE, (kv_heads + head + 1) * HEAD_SIZE),
        )

    steps = group // together
    for head in range(kv_heads):
        kcol, vcol = kv_cols(head)

        @pl.loop(0, steps)
        def _(step):
            cols, q = head_parts(head, step)
            keys = own_ref[:, :, kcol].reshape(own_len, HEAD_SIZE)
            values = own_ref[:, :, vcol].reshape(own_len, HEAD_SIZE)
            scores = lax.dot_general(q, keys, nt, preferred_element_type=F32) * scale + bias
            top = jnp.max(scores, axis=1, keepdims=True)
            p = jnp.exp(scores - top)
            tops[head * steps + step] = top
            totals[head * steps + step] = jnp.sum(p, axis=1, keepdims=True)
            mixed = jnp.dot(p.astype(BF16), values, preferred_element_type=F32)
            for i, c in enumerate(cols):
                state_ref[:, c] = mixed[i * rows : (i + 1) * rows]

    for copy in copies:
        copy.wait()
    for head in range(kv_heads):
        kcol, vcol = kv_cols(head)

        @pl.loop(0, steps)
        def _(step):
            cols, q = head_parts(head, step)
            keys = sib_ref[:, :, kcol].reshape(sib_len, HEAD_SIZE)
            values = sib_ref[:, :, vcol].reshape(sib_len, HEAD_SIZE)
            scores = lax.dot_general(q, keys, nt, preferred_element_type=F32) * scale
            own_top = tops[head * steps + step]
            top = jnp.maximum(own_top, jnp.max(scores, axis=1, keepdims=True))
            p = jnp.exp(scores - top)
            shrink = jnp.exp(own_top - top)
            total = totals[head * steps + step] * shrink + jnp.sum(p, axis=1, keepdims=True)
            mixed = jnp.dot(p.astype(BF16), values, preferred_element_type=F32)
            inverse = 1.0 / total
            for i, c in enumerate(cols):
                part = slice(i * rows, (i + 1) * rows)
                context = (state_ref[:, c] * shrink[part] + mixed[part]) * inverse[part]
                state_ref[:, c] = res_ref[:, c].astype(F32) + context.astype(BF16).astype(F32)

    state = state_ref[...]
    normed = (
        state * lax.rsqrt(jnp.mean(state * state, axis=1, keepdims=True) + 1e-06)
    ).astype(BF16)
    logits = lax.dot_general(normed, router_ref[...], nt, preferred_element_type=F32)

    top_count = ids_ref.shape[1]
    ids, idt = ids_ref[...], idt_ref[...]
    kinds = lax.broadcasted_iota(jnp.int32, (rows, experts), 1)
    kinds_t = lax.broadcasted_iota(jnp.int32, (experts, rows), 0)
    hot = [(ids[:, k : k + 1] == kinds).astype(F32) for k in range(top_count)]
    hot_t = [(idt[k : k + 1, :] == kinds_t).astype(F32) for k in range(top_count)]
    down = lax.broadcasted_iota(jnp.int32, (rows, rows), 0)
    along = lax.broadcasted_iota(jnp.int32, (rows, rows), 1)
    before = jnp.dot((along < down).astype(F32).astype(BF16), sum(hot).astype(BF16), preferred_element_type=F32)
    before_t = jnp.dot(sum(hot_t).astype(BF16), (down < along).astype(F32).astype(BF16), preferred_element_type=F32)
    dest, dest_t = [], []
    for k in range(top_count):
        slot = jnp.sum(before * hot[k], axis=1, keepdims=True).astype(jnp.int32)
        dest.append((ids[:, k : k + 1] ^ me) * cap + slot)
        slot_t = jnp.sum(before_t * hot_t[k], axis=0, keepdims=True).astype(jnp.int32)
        dest_t.append((idt[k : k + 1, :] ^ me) * cap + slot_t)
    chosen = [jnp.sum(logits * hot[k], axis=1, keepdims=True) for k in range(top_count)]
    gates = [1.0 / sum(jnp.exp(c - chosen[k]) for c in chosen) for k in range(top_count)]

    parts, _, part_width = norm_ref.shape
    for c in range(parts):
        norm_ref[c] = normed[:, c * part_width : (c + 1) * part_width]
    logits_t = lax.dot_general(router_ref[...], normed, nt, preferred_element_type=F32)
    chosen_t = [jnp.sum(logits_t * hot_t[k], axis=0, keepdims=True) for k in range(top_count)]
    meta_ref[...] = jnp.zeros_like(meta_ref)
    for k in range(top_count):
        meta_ref[k : k + 1, :] = dest_t[k].astype(F32)
        meta_ref[top_count + k : top_count + k + 1, :] = 1.0 / sum(
            jnp.exp(c - chosen_t[k]) for c in chosen_t
        )

    pair = 2 * cap
    places = lax.broadcasted_iota(jnp.int32, (rows, pair), 1)
    places_t = lax.broadcasted_iota(jnp.int32, (pair, rows), 0)
    for p in range(send_ref.shape[0] // pair):
        pick = sum((dest_t[k] - p * pair == places_t).astype(F32) for k in range(top_count))
        send_ref[p * pair : (p + 1) * pair, :] = jnp.dot(
            pick.astype(BF16), normed, preferred_element_type=F32
        ).astype(BF16)
        weight = sum(
            jnp.where(dest[k] - p * pair == places, gates[k], 0.0) for k in range(top_count)
        )
        high = weight.astype(BF16)
        gate_ref[p, 0] = high
        gate_ref[p, 1] = (weight - high.astype(F32)).astype(BF16)


def attend(listed, q, own, residual, router_t, ids, experts, near, cap, n_branch, n_seq):
    rows, width = q.shape
    halves = width // HEAD_SIZE // 2
    return pl.pallas_call(
        functools.partial(attend_kernel, experts, cap, n_branch, n_seq),
        out_shape=(
            jax.ShapeDtypeStruct((near * cap, width), BF16),
            jax.ShapeDtypeStruct((rows, width), F32),
            jax.ShapeDtypeStruct((near // 2, 2, rows, 2 * cap), BF16),
            jax.ShapeDtypeStruct((PARTS, rows, width // PARTS), BF16),
            jax.ShapeDtypeStruct((8, rows), F32),
        ),
        in_specs=[SMEM] + [VMEM] * 6,
        out_specs=(VMEM,) * 5,
        scratch_shapes=[
            pltpu.VMEM((n_branch - 1, rows, own.shape[2]), BF16),
            pltpu.VMEM((n_branch - 1, rows, own.shape[2]), BF16),
            pltpu.VMEM((halves, 2 * rows, 1), F32),
            pltpu.VMEM((halves, 2 * rows, 1), F32),
            pltpu.SemaphoreType.DMA((n_branch,)),
            pltpu.SemaphoreType.DMA((n_branch,)),
        ],
        compiler_params=pltpu.CompilerParams(
            collective_id=0, has_side_effects=True, vmem_limit_bytes=VMEM_LIMIT
        ),
    )(listed, q, own, residual, router_t, ids, ids.T)


def expert_kernel(
    experts, cap, n_seq,
    send_ref, state_ref, gate_ref, wgu_ref, wdn_ref, out_ref,
    recv, res, ret, wgu, wdn, acc,
    wsend, wrecv, wloc, lsem, dsend, drecv, bsend, brecv,
):
    branch = lax.axis_index("branch")
    seq = lax.axis_index("seq")
    core = seq % 2
    me = (branch * n_seq + seq) // 2
    pair = 2 * cap
    width = send_ref.shape[1]
    twin = {"seq": seq + 1 - 2 * core}
    mesh_id = pl.DeviceIdType.MESH

    def place(k):
        other = flipped(me, k, experts)
        return {"branch": (2 * other) // n_seq, "seq": (2 * other) % n_seq + core}

    barrier = pltpu.get_barrier_semaphore()
    pl.semaphore_signal(barrier, inc=1, device_id=twin, device_id_type=mesh_id)

    @pl.loop(1, experts)
    def _(k):
        pl.semaphore_signal(barrier, inc=1, device_id=place(k), device_id_type=mesh_id)

    pl.semaphore_wait(barrier, experts)

    def block(k):
        return pl.ds(pl.multiple_of(k * cap, 16), cap)

    def dispatch(k):
        return pltpu.make_async_remote_copy(
            src_ref=send_ref.at[block(k)], dst_ref=recv.at[block(k)],
            send_sem=dsend.at[k], recv_sem=drecv.at[k],
            device_id=place(k), device_id_type=mesh_id,
        )

    def give_back(k):
        return pltpu.make_async_remote_copy(
            src_ref=res.at[block(k)], dst_ref=ret.at[block(k)],
            send_sem=bsend.at[k], recv_sem=brecv.at[k],
            device_id=place(k), device_id_type=mesh_id,
        )

    weights = []
    for i, (src, dst) in enumerate(((wgu_ref, wgu), (wdn_ref, wdn))):
        weights.append(
            pltpu.make_async_remote_copy(
                src_ref=src, dst_ref=dst.at[1], send_sem=wsend.at[i], recv_sem=wrecv.at[i],
                device_id=twin, device_id_type=mesh_id,
            )
        )
        weights.append(pltpu.make_async_copy(src, dst.at[0], wloc.at[i]))
    dispatch(1).start()
    mine = pltpu.make_async_copy(send_ref.at[block(0)], recv.at[block(0)], lsem)
    mine.start()

    @pl.loop(experts // 2, experts)
    def _(k):
        dispatch(k).start()

    @pl.loop(2, experts // 2)
    def _(k):
        dispatch(k).start()

    for copy in weights:
        copy.start()
    acc[...] = state_ref[...]
    for copy in weights:
        copy.wait()

    chunk = 512

    def compute(p):
        span = pl.ds(pl.multiple_of(p * pair, 16), pair)
        acts = []
        for h in range(2):
            x = recv[span, :]
            gate = jnp.dot(x, wgu[h, 0], preferred_element_type=F32)
            up = jnp.dot(x, wgu[h, 1], preferred_element_type=F32)
            acts.append((gate / (1.0 + jnp.exp(-gate)) * up).astype(BF16))
        for start in range(0, width, chunk):
            cols = slice(start, start + chunk)
            done = jnp.dot(acts[0], wdn[0, :, cols], preferred_element_type=F32)
            done += jnp.dot(acts[1], wdn[1, :, cols], preferred_element_type=F32)
            res[span, cols] = done.astype(BF16)

    quarter = experts // 4

    def turn(i):
        return jnp.where(i <= quarter, i + quarter - 1, i - quarter)

    mine.wait()
    dispatch(1).wait_recv()
    compute(0)
    give_back(1).start()

    @pl.loop(1, experts // 2)
    def _(i):
        p = turn(i)
        dispatch(2 * p).wait_recv()
        dispatch(2 * p + 1).wait_recv()
        compute(p)
        give_back(2 * p).start()
        give_back(2 * p + 1).start()

    def add(p, rows):
        for start in range(0, width, chunk):
            cols = slice(start, start + chunk)
            block_rows = rows(cols)
            acc[:, cols] += jnp.dot(
                gate_ref[p, 0], block_rows, preferred_element_type=F32
            ) + jnp.dot(gate_ref[p, 1], block_rows, preferred_element_type=F32)

    give_back(1).wait_recv()
    add(0, lambda cols: jnp.concatenate([res[0:cap, cols], ret[cap:pair, cols]], axis=0))

    @pl.loop(1, experts // 2)
    def _(i):
        p = turn(i)
        give_back(2 * p).wait_recv()
        give_back(2 * p + 1).wait_recv()
        span = pl.ds(pl.multiple_of(p * pair, 16), pair)
        add(p, lambda cols: ret[span, cols])

    out_ref[...] = acc[...].astype(BF16)

    @pl.loop(1, experts)
    def _(k):
        dispatch(k).wait_send()
        give_back(k).wait_send()


def run_experts(send, state, gate, wgu, wdn, experts, cap, n_seq):
    rows, width = state.shape
    ff = wdn.shape[0]
    return pl.pallas_call(
        functools.partial(expert_kernel, experts, cap, n_seq),
        out_shape=jax.ShapeDtypeStruct((rows, width), BF16),
        in_specs=[ANY, VMEM, VMEM, ANY, ANY],
        out_specs=VMEM,
        scratch_shapes=[
            pltpu.VMEM((experts * cap, width), BF16),
            pltpu.VMEM((experts * cap, width), BF16),
            pltpu.VMEM((experts * cap, width), BF16),
            pltpu.VMEM((2, 2, width, ff), BF16),
            pltpu.VMEM((2, ff, width), BF16),
            pltpu.VMEM((rows, width), F32),
            pltpu.SemaphoreType.DMA((2,)),
            pltpu.SemaphoreType.DMA((2,)),
            pltpu.SemaphoreType.DMA((2,)),
            pltpu.SemaphoreType.DMA,
            pltpu.SemaphoreType.DMA((experts,)),
            pltpu.SemaphoreType.DMA((experts,)),
            pltpu.SemaphoreType.DMA((experts,)),
            pltpu.SemaphoreType.DMA((experts,)),
        ],
        compiler_params=pltpu.CompilerParams(
            collective_id=1, has_side_effects=True, vmem_limit_bytes=VMEM_LIMIT
        ),
    )(send, state, gate, wgu, wdn)


def relay_kernel(
    cap, n_seq,
    send_ref, state_ref, gate_ref, norm_ref, meta_ref, wgu_ref, wdn_ref, out_ref,
    recv, res, ret, wgu, wdn, acc, xin, xmeta, fwd, rbuf, xout, far,
    wsend, wrecv, wloc, lsem, dsend, drecv, bsend, brecv,
    csend, crecv, msend, mrecv, fsend, rsend, rrecv, osend, orecv,
):
    experts, near = 8, 4
    branch = lax.axis_index("branch")
    seq = lax.axis_index("seq")
    core = seq % 2
    me = (branch * n_seq + seq) // 2
    inner = (branch + 1) // 2 % 2
    pair = 2 * cap
    rows, width = state_ref.shape
    step = width // PARTS
    twin = {"seq": seq + 1 - 2 * core}
    mesh_id = pl.DeviceIdType.MESH

    def place(k):
        other = flipped(me, k, experts)
        return {"branch": (2 * other) // n_seq, "seq": (2 * other) % n_seq + core}

    barrier = pltpu.get_barrier_semaphore()
    pl.semaphore_signal(barrier, inc=1, device_id=twin, device_id_type=mesh_id)
    for k in range(1, experts):
        pl.semaphore_signal(barrier, inc=1, device_id=place(k), device_id_type=mesh_id)
    pl.semaphore_wait(barrier, experts)

    def block(k):
        return pl.ds(pl.multiple_of(k * cap, 16), cap)

    def remote(src, dst, send, arrive, k):
        return pltpu.make_async_remote_copy(
            src_ref=src, dst_ref=dst, send_sem=send, recv_sem=arrive,
            device_id=place(k), device_id_type=mesh_id,
        )

    def dispatch(k):
        return remote(send_ref.at[block(k)], recv.at[block(k)], dsend.at[k], drecv.at[k], k)

    def give_back(k):
        return remote(res.at[block(k)], ret.at[block(k)], bsend.at[k], brecv.at[k], k)

    across = 4 + 2 * inner

    def cross(c):
        return remote(norm_ref.at[c], xin.at[1 - inner, c], csend.at[c], crecv.at[1 - inner, c], across)

    def cross_meta():
        return remote(meta_ref, xmeta.at[1 - inner], msend, mrecv.at[1 - inner], across)

    def arrived(s, c):
        return remote(norm_ref.at[c], xin.at[s, c], csend.at[c], crecv.at[s, c], across)

    def slot_of(s, f):
        return f ^ (6 - 2 * s)

    def part(c):
        return slice(c * step, (c + 1) * step)

    def forward(s, f, c):
        k = slot_of(s, f)
        src = fwd.at[s, f, :, part(c)]
        dst = recv.at[block(k), part(c)]
        if f == 0:
            return pltpu.make_async_copy(src, dst, drecv.at[k])
        return remote(src, dst, fsend.at[s, f], drecv.at[k], f)

    def got(k):
        remote(recv.at[block(k)], recv.at[block(k)], dsend.at[k], drecv.at[k], 1).wait_recv()

    weights = []
    for i, (src, dst) in enumerate(((wgu_ref, wgu), (wdn_ref, wdn))):
        weights.append(
            pltpu.make_async_remote_copy(
                src_ref=src, dst_ref=dst.at[1], send_sem=wsend.at[i], recv_sem=wrecv.at[i],
                device_id=twin, device_id_type=mesh_id,
            )
        )
        weights.append(pltpu.make_async_copy(src, dst.at[0], wloc.at[i]))

    def start_cross():
        cross_meta().start()
        for c in range(PARTS):
            cross(c).start()

    pl.when(inner == 1)(start_cross)
    mine = pltpu.make_async_copy(send_ref.at[block(0)], recv.at[block(0)], lsem)
    mine.start()
    for k in (1, 2, 3):
        dispatch(k).start()
    pl.when(inner == 0)(start_cross)
    for copy in weights:
        copy.start()
    acc[...] = state_ref[...]

    def rows_of(s):
        where = lax.broadcasted_iota(jnp.int32, (cap, rows), 0).astype(F32)
        meta = xmeta[s]
        return meta, [where + float(slot_of(s, f) * cap) for f in range(near)]

    def relay(s):
        remote(meta_ref, xmeta.at[s], msend, mrecv.at[s], across).wait_recv()
        meta, where = rows_of(s)
        pick = jnp.concatenate(
            [(meta[0:1] == w).astype(F32) + (meta[1:2] == w).astype(F32) for w in where], axis=0
        ).astype(BF16)
        for c in range(PARTS):
            arrived(s, c).wait_recv()
            taken = jnp.dot(pick, xin[s, c], preferred_element_type=F32).astype(BF16)
            for f in range(near):
                fwd[s, f, :, part(c)] = taken[f * cap : (f + 1) * cap]
            for f in (2, 3, 1, 0):
                forward(s, f, c).start()

    def hand(s, f, c, k):
        src = res.at[block(k), part(c)]
        dst = rbuf.at[s, f, :, part(c)]
        if f == 0:
            return pltpu.make_async_copy(src, dst, rrecv.at[s, f, c])
        return remote(src, dst, rsend.at[s, f, c], rrecv.at[s, f, c], f)

    def compute(p, after=None):
        span = pl.ds(pl.multiple_of(p * pair, 16), pair)
        acts = []
        for h in range(2):
            x = recv[span, :]
            gate = jnp.dot(x, wgu[h, 0], preferred_element_type=F32)
            up = jnp.dot(x, wgu[h, 1], preferred_element_type=F32)
            acts.append((gate / (1.0 + jnp.exp(-gate)) * up).astype(BF16))
        for c in range(PARTS):
            done = jnp.dot(acts[0], wdn[0, :, part(c)], preferred_element_type=F32)
            done += jnp.dot(acts[1], wdn[1, :, part(c)], preferred_element_type=F32)
            res[span, part(c)] = done.astype(BF16)
            if after is not None:
                after(c)

    pl.when(inner == 1)(lambda: relay(0))
    for copy in weights:
        copy.wait()
    mine.wait()
    got(1)
    compute(0)
    give_back(1).start()
    got(2)
    got(3)
    compute(1)
    give_back(2).start()
    give_back(3).start()
    pl.when(inner == 1)(lambda: relay(1))

    def far_group(s, base):
        def after(c):
            for f in (base, base + 1):
                hand(s, f, c, slot_of(s, f)).start()

        k = slot_of(s, base) // 2 * 2
        got(k)
        got(k + 1)
        compute(k // 2, after)

    for s in range(2):
        pl.when(inner == 1)(functools.partial(far_group, s, 0))
        pl.when(inner == 0)(functools.partial(far_group, s, 2))

    def result(s, c):
        return remote(xout.at[s, c], far.at[c], osend.at[s, c], orecv.at[c], 6 - 2 * s)

    def combine(s):
        meta, where = rows_of(s)
        weight = jnp.concatenate(
            [
                jnp.where(meta[0:1] == w, meta[2:3], 0.0) + jnp.where(meta[1:2] == w, meta[3:4], 0.0)
                for w in where
            ],
            axis=0,
        ).T
        high = weight.astype(BF16)
        low = (weight - high.astype(F32)).astype(BF16)
        for c in range(PARTS):
            for f in range(near):
                if f == 0:
                    hand(s, 0, c, slot_of(s, 0)).wait()
                else:
                    hand(s, f, c, slot_of(s, f)).wait_recv()
            given = rbuf[s, :, :, part(c)].reshape(near * cap, step)
            xout[s, c] = (
                jnp.dot(high, given, preferred_element_type=F32)
                + jnp.dot(low, given, preferred_element_type=F32)
            ).astype(BF16)
            result(s, c).start()

    def combine_all():
        combine(0)
        combine(1)

    pl.when(inner == 1)(combine_all)

    for p in range(near // 2):
        for k in (2 * p, 2 * p + 1):
            if k:
                give_back(k).wait_recv()
        for c in range(PARTS):
            cols = part(c)
            low = res if p == 0 else ret
            given = jnp.concatenate(
                [low[2 * p * cap : (2 * p + 1) * cap, cols], ret[(2 * p + 1) * cap : (2 * p + 2) * cap, cols]],
                axis=0,
            )
            acc[:, cols] += jnp.dot(gate_ref[p, 0], given, preferred_element_type=F32) + jnp.dot(
                gate_ref[p, 1], given, preferred_element_type=F32
            )
    for c in range(PARTS):
        result(0, c).wait_recv()
        out_ref[:, part(c)] = (acc[:, part(c)] + far[c].astype(F32)).astype(BF16)

    for k in (1, 2, 3):
        dispatch(k).wait_send()
        give_back(k).wait_send()
    cross_meta().wait_send()
    for c in range(PARTS):
        cross(c).wait_send()

    def inner_end():
        for s in range(2):
            for f in (1, 2, 3):
                remote(fwd.at[s, f], fwd.at[s, f], fsend.at[s, f], drecv.at[0], f).wait_send()
            for c in range(PARTS):
                hand(s, 1, c, slot_of(s, 1)).wait_send()
                result(s, c).wait_send()

    def outer_end():
        for s in range(2):
            for f in (2, 3):
                for c in range(PARTS):
                    hand(s, f, c, slot_of(s, f)).wait_send()

    pl.when(inner == 1)(inner_end)
    pl.when(inner == 0)(outer_end)


def run_relayed(send, state, gate, normed, meta, wgu, wdn, cap, n_seq):
    rows, width = state.shape
    ff = wdn.shape[0]
    part = width // PARTS
    dma = pltpu.SemaphoreType.DMA
    return pl.pallas_call(
        functools.partial(relay_kernel, cap, n_seq),
        out_shape=jax.ShapeDtypeStruct((rows, width), BF16),
        in_specs=[ANY, VMEM, VMEM, ANY, VMEM, ANY, ANY],
        out_specs=VMEM,
        scratch_shapes=[
            pltpu.VMEM((8 * cap, width), BF16),
            pltpu.VMEM((8 * cap, width), BF16),
            pltpu.VMEM((4 * cap, width), BF16),
            pltpu.VMEM((2, 2, width, ff), BF16),
            pltpu.VMEM((2, ff, width), BF16),
            pltpu.VMEM((rows, width), F32),
            pltpu.VMEM((2, PARTS, rows, part), BF16),
            pltpu.VMEM((2, 8, rows), F32),
            pltpu.VMEM((2, 4, cap, width), BF16),
            pltpu.VMEM((2, 4, cap, width), BF16),
            pltpu.VMEM((2, PARTS, rows, part), BF16),
            pltpu.VMEM((PARTS, rows, part), BF16),
            dma((2,)), dma((2,)), dma((2,)), dma,
            dma((8,)), dma((8,)), dma((8,)), dma((8,)),
            dma((PARTS,)), dma((2, PARTS)), dma, dma((2,)), dma((2, 4)),
            dma((2, 4, PARTS)), dma((2, 4, PARTS)), dma((2, PARTS)), dma((PARTS,)),
        ],
        compiler_params=pltpu.CompilerParams(
            collective_id=2, has_side_effects=True, vmem_limit_bytes=VMEM_LIMIT
        ),
    )(send, state, gate, normed, meta, wgu, wdn)


def on_device(
    n_branch, n_seq, queries, keyvals, residual, read_list, router, expert_ids, w_gate_up, w_down
):
    rows = queries.shape[1]
    experts = router.shape[1]
    top_count = expert_ids.shape[2]
    capacity = 2 * ((3 * rows * top_count + 4 * experts - 1) // (4 * experts))
    cap = (capacity + 15) // 16 * 16
    kv = keyvals.reshape(rows, -1)
    shifts = [
        lax.ppermute(kv, "seq", [(i, (i + step) % n_seq) for i in range(n_seq)])
        for step in range(1, n_seq)
    ]
    own = jnp.stack([kv] + shifts)
    wgu = jnp.swapaxes(w_gate_up[0], 0, 1)
    line = n_branch == 4 and n_seq == 4 and experts == 8 and top_count == 2
    near = 4 if line else experts
    send, state, gate, normed, meta = attend(
        read_list.reshape(-1), queries[0], own, residual[0], router.T, expert_ids[0],
        experts, near, cap, n_branch, n_seq,
    )
    if line:
        return run_relayed(send, state, gate, normed, meta, wgu, w_down[0], cap, n_seq)[None]
    return run_experts(send, state, gate, wgu, w_down[0], experts, cap, n_seq)[None]


def solution(mesh):
    return jax.shard_map(
        functools.partial(on_device, mesh.shape["branch"], mesh.shape["seq"]),
        mesh=mesh,
        in_specs=(
            P(("rollout", "branch"), "seq", None),
            P(("rollout", "branch"), "seq", None, None),
            P(("rollout", "branch"), "seq", None),
            P(("rollout", "branch"), "seq", None),
            P(),
            P(("rollout", "branch"), "seq", None),
            P(("branch", "seq"), None, None, None),
            P(("branch", "seq"), None, None),
        ),
        out_specs=P(("rollout", "branch"), "seq", None),
        check_vma=False,
    )
```

profile of v0, /device:TPU:0, one launch (start us, length us, event | category | flops | bytes accessed | tf_op | source)
XLA Modules:
  0.0 188.0 jit_solution(17547731840055901950)
XLA Ops:
  0.0 0.9 copy.11
  0.9 2.5 %collective-permute-start.2 = (bf16[128,512]{1,0:T(8,128)(2,1)S(1)}, bf16[128,512]{1,0:T(8,128)(2,1)S(1)}, u32[]{:S(2)}, u32[]{:S(2)}) collective-permute-start(bf16[128,512]{1,0:T(8,128)(2,1)S(1)} %bitcast.26), channel_id=1, source_target_pairs={{0,3},{1,0},{2,1},{3,2},{4,7},{5,4},{6,5},{7,6},{8,11},{9,8},{10,9... | collective-permute-start | bytes 393224 | tf_op jit(solution)/shard_map/ppermute | solution.py:663
  3.4 0.6 collective-permute-start.1
  4.0 0.2 collective-permute-start
  4.2 1.0 stack_reshape.3
  5.2 1.4 copy.9.ids_ref
  6.6 6.2 %copy.13 = bf16[1,4096,2,384]{3,1,2,0:T(8,128)(2,1)} copy(bf16[1,4096,2,384]{3,2,1,0:T(2,128)(2,1)} %param.14) | data formatting | bytes 12582912 | tf_op args[6]
  12.8 0.0 collective-permute-done.2
  12.8 0.0 collective-permute-done.1
  12.8 0.0 collective-permute-done
  12.8 0.9 pad_maximum_fusion.own_ref
  13.7 27.5 %shard_map.82 = (bf16[192,4096]{1,0:T(8,128)(2,1)}, f32[128,4096]{1,0:T(8,128)}, bf16[2,2,128,96]{3,2,1,0:T(8,128)(2,1)}, bf16[4,128,1024]{2,1,0:T(8,128)(2,1)}, f32[8,128]{1,0:T(8,128)}) custom-call(s32[3]{0:T(128)} %bitcast.35, bf16[128,4096]{1,0:T(8,128)(2,1)} %bitcast.23, bf16[4,128,512]{2,1,0:T(8,128)(2,1)} %pad_maximum_fusion.own_ref, ...), custom_call_target="tpu_custom_call" | custom-call | tf_op jit(solution)/shard_map/pallas_call | solution.py:188
  41.2 144.5 %shard_map.83 = bf16[128,4096]{1,0:T(8,128)(2,1)} custom-call(bf16[192,4096]{1,0:T(8,128)(2,1)} %get-tuple-element.10.send_ref, f32[128,4096]{1,0:T(8,128)} %get-tuple-element.11.state_ref, bf16[2,2,128,96]{3,2,1,0:T(8,128)(2,1)} %get-tuple-element.12.gate_ref, bf16[4,128,1024]{2,1,0:T(8,128)(2,1)} %get-tuple-element.13.norm_ref, ...), custom_call_target="tpu_custom_call" | custom-call | tf_op jit(solution)/shard_map/pallas_call | solution.py:624
  185.7 2.3 %copy.15 = bf16[1,128,4096]{2,1,0:T(8,128)(2,1)} copy(bf16[1,128,4096]{2,1,0:T(8,128)(2,1)} %bitcast.21) | data formatting | bytes 2097152
Async XLA Ops:
  0.9 11.9 %collective-permute-start.2 = (bf16[128,512]{1,0:T(8,128)(2,1)S(1)}, bf16[128,512]{1,0:T(8,128)(2,1)S(1)}, u32[]{:S(2)}, u32[]{:S(2)}) collective-permute-start(bf16[128,512]{1,0:T(8,128)(2,1)S(1)} %bitcast.26), channel_id=1, source_target_pairs={{0,3},{1,0},{2,1},{3,2},{4,7},{5,4},{6,5},{7,6},{8,11},{9,8},{10,9... | collective-permute-start | bytes 393224 | tf_op jit(solution)/shard_map/ppermute | solution.py:663
  3.4 9.4 %collective-permute-start.1 = (bf16[128,512]{1,0:T(8,128)(2,1)S(1)}, bf16[128,512]{1,0:T(8,128)(2,1)S(1)}, u32[]{:S(2)}, u32[]{:S(2)}) collective-permute-start(bf16[128,512]{1,0:T(8,128)(2,1)S(1)} %bitcast.27), channel_id=1, source_target_pairs={{0,2},{1,3},{2,0},{3,1},{4,6},{5,7},{6,4},{7,5},{8,10},{9,11},{10,... | collective-permute-start | bytes 393224 | tf_op jit(solution)/shard_map/ppermute | solution.py:663
  4.0 8.8 %collective-permute-start = (bf16[128,512]{1,0:T(8,128)(2,1)S(1)}, bf16[128,512]{1,0:T(8,128)(2,1)S(1)}, u32[]{:S(2)}, u32[]{:S(2)}) collective-permute-start(bf16[128,512]{1,0:T(8,128)(2,1)S(1)} %bitcast.28), channel_id=1, source_target_pairs={{0,1},{1,2},{2,3},{3,0},{4,5},{5,6},{6,7},{7,4},{8,9},{9,10},{10,1... | collective-permute-start | bytes 393224 | tf_op jit(solution)/shard_map/ppermute | solution.py:663
where the time goes:
time: 188 us
  Pallas kernels  172 us (91%)
  local copies, waits for them, and re-layouts  11.8 us (6%)
  starting transfers between devices  3.25 us (2%)
    pallas_call x1, Pallas kernels, run_relayed(): pl.pallas_call(functools.partial(relay_kernel, cap, n_seq), out_shape=jax...  144 us
    pallas_call x1, Pallas kernels, attend(): pl.pallas_call(functools.partial(attend_kernel, experts, cap, n_branch, n...  27.5 us
    unnamed x3, local copies, waits for them, and re-layouts  9.44 us
  transfers between devices with their start and end apart: 3, of which 0 were waited for; matrix products, arithmetic and copies ran while one was open for 5% of the time, Pallas kernels for 0%

commit v1 on v0

--- a/solution.py
+++ b/solution.py
@@ -10,6 +10,7 @@
 
 HEAD_SIZE = 128
 PARTS = 4
+CHUNKS = 4
 VMEM_LIMIT = 60 * 1024 * 1024
 F32 = jnp.float32
 BF16 = jnp.bfloat16
@@ -374,280 +375,482 @@
     )(send, state, gate, wgu, wdn)
 
 
-def relay_kernel(
-    cap, n_seq,
-    send_ref, state_ref, gate_ref, norm_ref, meta_ref, wgu_ref, wdn_ref, out_ref,
-    recv, res, ret, wgu, wdn, acc, xin, xmeta, fwd, rbuf, xout, far,
-    wsend, wrecv, wloc, lsem, dsend, drecv, bsend, brecv,
-    csend, crecv, msend, mrecv, fsend, rsend, rrecv, osend, orecv,
+def line_kernel(
+    experts, cap, n_branch, n_seq,
+    list_ref, q_ref, kv_ref, res_ref, router_ref, idt_ref, wgu_ref, wdn_ref,
+    out_ref,
+    own, picked, sib, tops, totals, state, norm, raw, meta, xmeta,
+    recv, res, back, fwd, wgu, wdn, xout, fin,
+    kloc, ksend, krecv, ssend, srecv, wsend, wrecv, wloc,
+    rowsend, rowrecv, relsend, relrecv, msend, mrecv,
+    fsend, drecv, bsend, brecv, osend, orecv,
 ):
-    experts, near = 8, 4
     branch = lax.axis_index("branch")
     seq = lax.axis_index("seq")
-    core = seq % 2
-    me = (branch * n_seq + seq) // 2
     inner = (branch + 1) // 2 % 2
-    pair = 2 * cap
-    rows, width = state_ref.shape
+    mesh_id = pl.DeviceIdType.MESH
+    rows, width = q_ref.shape
+    kv_heads = own.shape[2] // (2 * HEAD_SIZE)
+    group = width // HEAD_SIZE // kv_heads
+    own_len = n_seq * rows
+    sib_len = (n_branch - 1) * rows
+    scale = 1.0 / math.sqrt(HEAD_SIZE)
+    nt = (((1,), (1,)), ((), ()))
     step = width // PARTS
-    twin = {"seq": seq + 1 - 2 * core}
-    mesh_id = pl.DeviceIdType.MESH
-
-    def place(k):
-        other = flipped(me, k, experts)
-        return {"branch": (2 * other) // n_seq, "seq": (2 * other) % n_seq + core}
-
-    barrier = pltpu.get_barrier_semaphore()
-    pl.semaphore_signal(barrier, inc=1, device_id=twin, device_id_type=mesh_id)
-    for k in range(1, experts):
-        pl.semaphore_signal(barrier, inc=1, device_id=place(k), device_id_type=mesh_id)
-    pl.semaphore_wait(barrier, experts)
-
-    def block(k):
-        return pl.ds(pl.multiple_of(k * cap, 16), cap)
-
-    def remote(src, dst, send, arrive, k):
+    span = rows // CHUNKS
+    pack = 2 * rows // span
+    halves = group // pack
+
+    across = (seq + 2) % n_seq
+    near = branch + 1 - 2 * (branch % 2)
+    far = n_branch - 1 - branch
+    onward = near + inner * (far - near)
+    places = [
+        {"branch": branch, "seq": seq},
+        {"branch": branch, "seq": across},
+        {"branch": near, "seq": seq},
+        {"branch": near, "seq": across},
+    ]
+    holders = [(p["branch"] * n_seq + p["seq"]) // 2 for p in places]
+
+    def remote(src, dst, send, arrive, device):
         return pltpu.make_async_remote_copy(
             src_ref=src, dst_ref=dst, send_sem=send, recv_sem=arrive,
-            device_id=place(k), device_id_type=mesh_id,
-        )
-
-    def dispatch(k):
-        return remote(send_ref.at[block(k)], recv.at[block(k)], dsend.at[k], drecv.at[k], k)
-
-    def give_back(k):
-        return remote(res.at[block(k)], ret.at[block(k)], bsend.at[k], brecv.at[k], k)
-
-    across = 4 + 2 * inner
-
-    def cross(c):
-        return remote(norm_ref.at[c], xin.at[1 - inner, c], csend.at[c], crecv.at[1 - inner, c], across)
-
-    def cross_meta():
-        return remote(meta_ref, xmeta.at[1 - inner], msend, mrecv.at[1 - inner], across)
-
-    def arrived(s, c):
-        return remote(norm_ref.at[c], xin.at[s, c], csend.at[c], crecv.at[s, c], across)
-
-    def slot_of(s, f):
-        return f ^ (6 - 2 * s)
+            device_id=device, device_id_type=mesh_id,
+        )
 
     def part(c):
         return slice(c * step, (c + 1) * step)
 
-    def forward(s, f, c):
-        k = slot_of(s, f)
-        src = fwd.at[s, f, :, part(c)]
-        dst = recv.at[block(k), part(c)]
-        if f == 0:
-            return pltpu.make_async_copy(src, dst, drecv.at[k])
-        return remote(src, dst, fsend.at[s, f], drecv.at[k], f)
-
-    def got(k):
-        remote(recv.at[block(k)], recv.at[block(k)], dsend.at[k], drecv.at[k], 1).wait_recv()
-
+    twin = {"seq": seq + 1 - 2 * (seq % 2)}
     weights = []
     for i, (src, dst) in enumerate(((wgu_ref, wgu), (wdn_ref, wdn))):
-        weights.append(
-            pltpu.make_async_remote_copy(
-                src_ref=src, dst_ref=dst.at[1], send_sem=wsend.at[i], recv_sem=wrecv.at[i],
-                device_id=twin, device_id_type=mesh_id,
-            )
-        )
         weights.append(pltpu.make_async_copy(src, dst.at[0], wloc.at[i]))
-
-    def start_cross():
-        cross_meta().start()
-        for c in range(PARTS):
-            cross(c).start()
-
-    pl.when(inner == 1)(start_cross)
-    mine = pltpu.make_async_copy(send_ref.at[block(0)], recv.at[block(0)], lsem)
+        weights.append(remote(src, dst.at[1], wsend.at[i], wrecv.at[i], twin))
+    mine = pltpu.make_async_copy(kv_ref, own.at[0], kloc)
     mine.start()
-    for k in (1, 2, 3):
-        dispatch(k).start()
-    pl.when(inner == 0)(start_cross)
+
+    barrier = pltpu.get_barrier_semaphore()
+    for shift in range(1, n_branch):
+        pl.semaphore_signal(
+            barrier, inc=1, device_id={"branch": (branch + shift) % n_branch}, device_id_type=mesh_id
+        )
+    for shift in range(1, n_seq):
+        pl.semaphore_signal(
+            barrier, inc=1, device_id={"seq": (seq + shift) % n_seq}, device_id_type=mesh_id
+        )
+    pl.semaphore_wait(barrier, n_branch + n_seq - 2)
+
+    def share(shift):
+        return remote(
+            kv_ref, own.at[shift], ksend.at[shift - 1], krecv.at[shift - 1],
+            {"seq": (seq + shift) % n_seq},
+        )
+
+    for shift in range(1, n_seq):
+        share(shift).start()
     for copy in weights:
         copy.start()
-    acc[...] = state_ref[...]
-
-    def rows_of(s):
+
+    idt = idt_ref[...]
+    top_count = idt.shape[0]
+    kinds_t = lax.broadcasted_iota(jnp.int32, (experts, rows), 0)
+    hot_t = [(idt[k : k + 1, :] == kinds_t).astype(F32) for k in range(top_count)]
+    down = lax.broadcasted_iota(jnp.int32, (rows, rows), 0)
+    along = lax.broadcasted_iota(jnp.int32, (rows, rows), 1)
+    before_t = jnp.dot(
+        sum(hot_t).astype(BF16), (down < along).astype(F32).astype(BF16), preferred_element_type=F32
+    )
+    meta[...] = jnp.zeros_like(meta)
+    for k in range(top_count):
+        slot_t = jnp.sum(before_t * hot_t[k], axis=0, keepdims=True)
+        meta[k : k + 1, :] = idt[k : k + 1, :].astype(F32) * float(cap) + slot_t
+
+    mine.wait()
+    for shift in range(1, n_seq):
+        share(shift).wait_recv()
+    for offset in range(n_branch - 1):
+        picked[offset] = own[(seq - list_ref[offset] + n_seq) % n_seq]
+
+    def lend(offset):
+        return remote(
+            picked.at[offset], sib.at[offset], ssend.at[offset], srecv.at[offset],
+            {"branch": (branch + offset + 1) % n_branch},
+        )
+
+    for offset in range(n_branch - 1):
+        lend(offset).start()
+
+    def chunk(r):
+        return pl.ds(pl.multiple_of(r * span, span), span)
+
+    def columns(head, half):
+        base = (head * group + half * pack) * HEAD_SIZE
+        return [slice(base + i * HEAD_SIZE, base + (i + 1) * HEAD_SIZE) for i in range(pack)]
+
+    def kv_cols(head):
+        return (
+            slice(head * HEAD_SIZE, (head + 1) * HEAD_SIZE),
+            slice((kv_heads + head) * HEAD_SIZE, (kv_heads + head + 1) * HEAD_SIZE),
+        )
+
+    tall = pack * span
+
+    @pl.loop(0, CHUNKS)
+    def _(r):
+        at_row = r * span + lax.broadcasted_iota(jnp.int32, (tall, own_len), 0) % span
+        at_col = lax.broadcasted_iota(jnp.int32, (tall, own_len), 1)
+        earlier = at_col // rows
+        bias = jnp.where(
+            earlier == 0,
+            jnp.where(at_col <= at_row, 0.0, -1e30),
+            jnp.where(earlier <= seq, 0.0, -1e30),
+        )
+        for head in range(kv_heads):
+            kcol, vcol = kv_cols(head)
+            for half in range(halves):
+                cols = columns(head, half)
+                q = jnp.concatenate([q_ref[chunk(r), c] for c in cols], axis=0)
+                keys = own[:, :, kcol].reshape(own_len, HEAD_SIZE)
+                values = own[:, :, vcol].reshape(own_len, HEAD_SIZE)
+                scores = lax.dot_general(q, keys, nt, preferred_element_type=F32) * scale + bias
+                top = jnp.max(scores, axis=1, keepdims=True)
+                p = jnp.exp(scores - top)
+                tops[r, head * halves + half] = top
+                totals[r, head * halves + half] = jnp.sum(p, axis=1, keepdims=True)
+                mixed = jnp.dot(p.astype(BF16), values, preferred_element_type=F32)
+                for i, c in enumerate(cols):
+                    state[chunk(r), c] = mixed[i * span : (i + 1) * span]
+
+    for offset in range(n_branch - 1):
+        lend(offset).wait_recv()
+
+    def rows_out(r):
+        return remote(
+            norm.at[chunk(r)], raw.at[inner, chunk(r)], rowsend.at[r], rowrecv.at[inner, r],
+            {"branch": onward},
+        )
+
+    @pl.loop(0, CHUNKS)
+    def _(r):
+        for head in range(kv_heads):
+            kcol, vcol = kv_cols(head)
+            for half in range(halves):
+                cols = columns(head, half)
+                q = jnp.concatenate([q_ref[chunk(r), c] for c in cols], axis=0)
+                keys = sib[:, :, kcol].reshape(sib_len, HEAD_SIZE)
+                values = sib[:, :, vcol].reshape(sib_len, HEAD_SIZE)
+                scores = lax.dot_general(q, keys, nt, preferred_element_type=F32) * scale
+                own_top = tops[r, head * halves + half]
+                top = jnp.maximum(own_top, jnp.max(scores, axis=1, keepdims=True))
+                p = jnp.exp(scores - top)
+                shrink = jnp.exp(own_top - top)
+                total = totals[r, head * halves + half] * shrink + jnp.sum(p, axis=1, keepdims=True)
+                mixed = jnp.dot(p.astype(BF16), values, preferred_element_type=F32)
+                inverse = 1.0 / total
+                for i, c in enumerate(cols):
+                    at = slice(i * span, (i + 1) * span)
+                    context = (state[chunk(r), c] * shrink[at] + mixed[at]) * inverse[at]
+                    state[chunk(r), c] = res_ref[chunk(r), c].astype(F32) + context.astype(BF16).astype(F32)
+        full = state[chunk(r), :]
+        norm[chunk(r), :] = (
+            full * lax.rsqrt(jnp.mean(full * full, axis=1, keepdims=True) + 1e-06)
+        ).astype(BF16)
+        rows_out(r).start()
+
+    logits_t = lax.dot_general(router_ref[...], norm[...], nt, preferred_element_type=F32)
+    chosen_t = [jnp.sum(logits_t * hot_t[k], axis=0, keepdims=True) for k in range(top_count)]
+    for k in range(top_count):
+        meta[top_count + k : top_count + k + 1, :] = 1.0 / sum(
+            jnp.exp(c - chosen_t[k]) for c in chosen_t
+        )
+
+    def meta_out():
+        return remote(meta, xmeta.at[inner], msend.at[0], mrecv.at[inner], {"branch": onward})
+
+    meta_out().start()
+
+    def relay(c):
+        return remote(
+            raw.at[0, :, part(c)], raw.at[2, :, part(c)], relsend.at[c], relrecv.at[c], {"branch": far}
+        )
+
+    def meta_relay():
+        return remote(xmeta.at[0], xmeta.at[2], msend.at[1], mrecv.at[2], {"branch": far})
+
+    def meta_of(g):
+        return meta[...] if g == 0 else xmeta[g - 1]
+
+    def slots_of(g, count):
         where = lax.broadcasted_iota(jnp.int32, (cap, rows), 0).astype(F32)
-        meta = xmeta[s]
-        return meta, [where + float(slot_of(s, f) * cap) for f in range(near)]
-
-    def relay(s):
-        remote(meta_ref, xmeta.at[s], msend, mrecv.at[s], across).wait_recv()
-        meta, where = rows_of(s)
-        pick = jnp.concatenate(
-            [(meta[0:1] == w).astype(F32) + (meta[1:2] == w).astype(F32) for w in where], axis=0
+        given = meta_of(g)
+        return given, [where + (holders[f] * cap).astype(F32) for f in range(count)]
+
+    def picks(g, count):
+        given, where = slots_of(g, count)
+        return jnp.concatenate(
+            [(given[0:1] == w).astype(F32) + (given[1:2] == w).astype(F32) for w in where], axis=0
         ).astype(BF16)
+
+    def shares(g, count):
+        given, where = slots_of(g, count)
+        weight = jnp.concatenate(
+            [
+                jnp.where(given[0:1] == w, given[2:3], 0.0) + jnp.where(given[1:2] == w, given[3:4], 0.0)
+                for w in where
+            ],
+            axis=0,
+        ).T
+        high = weight.astype(BF16)
+        return high, (weight - high.astype(F32)).astype(BF16)
+
+    def spot(g, f):
+        if f == 1:
+            return g, 1
+        return (1 if g == 0 else g), f - 2
+
+    def forward(g, f, c):
+        tg, th = spot(g, f)
+        return remote(
+            fwd.at[g, f - 1, :, part(c)], recv.at[tg, th, :, part(c)],
+            fsend.at[g, f - 1], drecv.at[tg, th], places[f],
+        )
+
+    def give(g, count, pick, c):
+        source = norm[:, part(c)] if g == 0 else raw[g - 1, :, part(c)]
+        taken = jnp.dot(pick, source, preferred_element_type=F32).astype(BF16)
+        recv[g, 0, :, part(c)] = taken[:cap]
+        for f in range(1, count):
+            fwd[g, f - 1, :, part(c)] = taken[f * cap : (f + 1) * cap]
+        for f in ((3, 2, 1) if count == 4 else (1,)):
+            forward(g, f, c).start()
+
+    def give_all(g, count):
+        pick = picks(g, count)
         for c in range(PARTS):
-            arrived(s, c).wait_recv()
-            taken = jnp.dot(pick, xin[s, c], preferred_element_type=F32).astype(BF16)
-            for f in range(near):
-                fwd[s, f, :, part(c)] = taken[f * cap : (f + 1) * cap]
-            for f in (2, 3, 1, 0):
-                forward(s, f, c).start()
-
-    def hand(s, f, c, k):
-        src = res.at[block(k), part(c)]
-        dst = rbuf.at[s, f, :, part(c)]
-        if f == 0:
-            return pltpu.make_async_copy(src, dst, rrecv.at[s, f, c])
-        return remote(src, dst, rsend.at[s, f, c], rrecv.at[s, f, c], f)
-
-    def compute(p, after=None):
-        span = pl.ds(pl.multiple_of(p * pair, 16), pair)
+            give(g, count, pick, c)
+
+    def whole(g, h):
+        return remote(recv.at[g, h], recv.at[g, h], fsend.at[0, 0], drecv.at[g, h], places[1])
+
+    def home(g, f, c):
+        if f == 1:
+            return g, 0
+        return (0 if g == 1 else g), f - 1
+
+    def hand(g, f, c):
+        tg, slot = home(g, f, c)
+        h = 1 if f == 1 else f - 2
+        return remote(
+            res.at[g, h, :, part(c)], back.at[tg, slot, :, part(c)],
+            bsend.at[g, h], brecv.at[tg, slot, c], places[f],
+        )
+
+    def compute(g):
+        whole(g, 1).wait_recv()
+        if g:
+            pl.when(inner == 0)(lambda: whole(g, 0).wait_recv())
+        x = recv[g].reshape(2 * cap, width)
         acts = []
         for h in range(2):
-            x = recv[span, :]
             gate = jnp.dot(x, wgu[h, 0], preferred_element_type=F32)
             up = jnp.dot(x, wgu[h, 1], preferred_element_type=F32)
             acts.append((gate / (1.0 + jnp.exp(-gate)) * up).astype(BF16))
         for c in range(PARTS):
             done = jnp.dot(acts[0], wdn[0, :, part(c)], preferred_element_type=F32)
             done += jnp.dot(acts[1], wdn[1, :, part(c)], preferred_element_type=F32)
-            res[span, part(c)] = done.astype(BF16)
-            if after is not None:
-                after(c)
-
-    pl.when(inner == 1)(lambda: relay(0))
+            res[g, :, :, part(c)] = done.astype(BF16).reshape(2, cap, step)
+            if g == 0:
+                hand(0, 1, c).start()
+            else:
+
+                def side():
+                    hand(g, 1, c).start()
+
+                def up_line():
+                    hand(g, 3, c).start()
+                    hand(g, 2, c).start()
+
+                pl.when(inner == 1)(side)
+                pl.when(inner == 0)(up_line)
+
+    def combined(g, count, weight, c):
+        for f in range(count - 1):
+            remote(
+                back.at[g, f, :, part(c)], back.at[g, f, :, part(c)],
+                bsend.at[0, 0], brecv.at[g, f, c], places[1],
+            ).wait_recv()
+        given = jnp.concatenate(
+            [res[g, 0, :, part(c)]] + [back[g, f, :, part(c)] for f in range(count - 1)], axis=0
+        )
+        return jnp.dot(weight[0], given, preferred_element_type=F32) + jnp.dot(
+            weight[1], given, preferred_element_type=F32
+        )
+
+    def result(s, c):
+        if s == 2:
+            return remote(xout.at[2, c], fin.at[0, c], osend.at[2, c], orecv.at[0, c], {"branch": near})
+        return remote(xout.at[s, c], fin.at[s, c], osend.at[s, c], orecv.at[s, c], {"branch": far})
+
+    def wait_rows(g):
+        remote(xmeta.at[g - 1], xmeta.at[g - 1], msend.at[0], mrecv.at[g - 1], places[2]).wait_recv()
+        if g < 3:
+            for r in range(CHUNKS):
+                at = slice(r * span, (r + 1) * span)
+                remote(
+                    raw.at[g - 1, at], raw.at[g - 1, at], rowsend.at[0], rowrecv.at[g - 1, r], places[2]
+                ).wait_recv()
+
+    is_inner = pl.when(inner == 1)
+    is_outer = pl.when(inner == 0)
+
+    is_inner(lambda: give_all(0, 4))
+    is_outer(lambda: give_all(0, 2))
+
     for copy in weights:
         copy.wait()
-    mine.wait()
-    got(1)
     compute(0)
-    give_back(1).start()
-    got(2)
-    got(3)
+
+    @is_inner
+    def _():
+        wait_rows(1)
+        for c in range(PARTS):
+            relay(c).start()
+        meta_relay().start()
+        wait_rows(2)
+        give_all(2, 4)
+        give_all(1, 2)
+
     compute(1)
-    give_back(2).start()
-    give_back(3).start()
-    pl.when(inner == 1)(lambda: relay(1))
-
-    def far_group(s, base):
-        def after(c):
-            for f in (base, base + 1):
-                hand(s, f, c, slot_of(s, f)).start()
-
-        k = slot_of(s, base) // 2 * 2
-        got(k)
-        got(k + 1)
-        compute(k // 2, after)
-
-    for s in range(2):
-        pl.when(inner == 1)(functools.partial(far_group, s, 0))
-        pl.when(inner == 0)(functools.partial(far_group, s, 2))
-
-    def result(s, c):
-        return remote(xout.at[s, c], far.at[c], osend.at[s, c], orecv.at[c], 6 - 2 * s)
-
-    def combine(s):
-        meta, where = rows_of(s)
-        weight = jnp.concatenate(
-            [
-                jnp.where(meta[0:1] == w, meta[2:3], 0.0) + jnp.where(meta[1:2] == w, meta[3:4], 0.0)
-                for w in where
-            ],
-            axis=0,
-        ).T
-        high = weight.astype(BF16)
-        low = (weight - high.astype(F32)).astype(BF16)
+
+    def far_rows(c):
+        relay_in = remote(
+            raw.at[2, :, part(c)], raw.at[2, :, part(c)], relsend.at[0], relrecv.at[c], places[2]
+        )
+        relay_in.wait_recv()
+
+    @is_inner
+    def _():
+        wait_rows(3)
+        pick = picks(3, 4)
         for c in range(PARTS):
-            for f in range(near):
-                if f == 0:
-                    hand(s, 0, c, slot_of(s, 0)).wait()
-                else:
-                    hand(s, f, c, slot_of(s, f)).wait_recv()
-            given = rbuf[s, :, :, part(c)].reshape(near * cap, step)
-            xout[s, c] = (
-                jnp.dot(high, given, preferred_element_type=F32)
-                + jnp.dot(low, given, preferred_element_type=F32)
-            ).astype(BF16)
-            result(s, c).start()
-
-    def combine_all():
-        combine(0)
-        combine(1)
-
-    pl.when(inner == 1)(combine_all)
-
-    for p in range(near // 2):
-        for k in (2 * p, 2 * p + 1):
-            if k:
-                give_back(k).wait_recv()
+            far_rows(c)
+            give(3, 4, pick, c)
+
+    compute(2)
+    compute(3)
+
+    @is_inner
+    def _():
+        for s in range(2):
+            weight = shares(2 + s, 4)
+            for c in range(PARTS):
+                xout[s, c] = combined(2 + s, 4, weight, c).astype(BF16)
+                result(s, c).start()
+        weight = shares(0, 4)
         for c in range(PARTS):
-            cols = part(c)
-            low = res if p == 0 else ret
-            given = jnp.concatenate(
-                [low[2 * p * cap : (2 * p + 1) * cap, cols], ret[(2 * p + 1) * cap : (2 * p + 2) * cap, cols]],
-                axis=0,
-            )
-            acc[:, cols] += jnp.dot(gate_ref[p, 0], given, preferred_element_type=F32) + jnp.dot(
-                gate_ref[p, 1], given, preferred_element_type=F32
-            )
+            state[:, part(c)] += combined(0, 4, weight, c)
+
+    @is_outer
+    def _():
+        weight = shares(0, 2)
+        for c in range(PARTS):
+            state[:, part(c)] += combined(0, 2, weight, c)
+
+    def arrived(s, c):
+        remote(fin.at[s, c], fin.at[s, c], osend.at[0, 0], orecv.at[s, c], places[2]).wait_recv()
+
     for c in range(PARTS):
-        result(0, c).wait_recv()
-        out_ref[:, part(c)] = (acc[:, part(c)] + far[c].astype(F32)).astype(BF16)
-
-    for k in (1, 2, 3):
-        dispatch(k).wait_send()
-        give_back(k).wait_send()
-    cross_meta().wait_send()
-    for c in range(PARTS):
-        cross(c).wait_send()
-
-    def inner_end():
-        for s in range(2):
-            for f in (1, 2, 3):
-                remote(fwd.at[s, f], fwd.at[s, f], fsend.at[s, f], drecv.at[0], f).wait_send()
-            for c in range(PARTS):
-                hand(s, 1, c, slot_of(s, 1)).wait_send()
+        arrived(0, c)
+        out_ref[:, part(c)] = (state[:, part(c)] + fin[0, c].astype(F32)).astype(BF16)
+
+    @is_inner
+    def _():
+        weight = shares(1, 2)
+        for c in range(PARTS):
+            partial = combined(1, 2, weight, c)
+            arrived(1, c)
+            xout[2, c] = (partial + fin[1, c].astype(F32)).astype(BF16)
+            result(2, c).start()
+
+    for shift in range(1, n_seq):
+        share(shift).wait_send()
+    for offset in range(n_branch - 1):
+        lend(offset).wait_send()
+    for r in range(CHUNKS):
+        rows_out(r).wait_send()
+    meta_out().wait_send()
+
+    def sent(g, f):
+        remote(fwd.at[g, f - 1], fwd.at[g, f - 1], fsend.at[g, f - 1], drecv.at[0, 0], places[1]).wait_send()
+
+    def returned(g, h):
+        remote(res.at[g, h], res.at[g, h], bsend.at[g, h], brecv.at[0, 0, 0], places[1]).wait_send()
+
+    sent(0, 1)
+    returned(0, 1)
+
+    @is_inner
+    def _():
+        for g in (0, 2, 3):
+            for f in ((2, 3) if g == 0 else (1, 2, 3)):
+                sent(g, f)
+        sent(1, 1)
+        for g in (1, 2, 3):
+            returned(g, 1)
+        for c in range(PARTS):
+            relay(c).wait_send()
+            for s in range(3):
                 result(s, c).wait_send()
-
-    def outer_end():
-        for s in range(2):
-            for f in (2, 3):
-                for c in range(PARTS):
-                    hand(s, f, c, slot_of(s, f)).wait_send()
-
-    pl.when(inner == 1)(inner_end)
-    pl.when(inner == 0)(outer_end)
-
-
-def run_relayed(send, state, gate, normed, meta, wgu, wdn, cap, n_seq):
-    rows, width = state.shape
+        meta_relay().wait_send()
+
+    @is_outer
+    def _():
+        for g in (1, 2, 3):
+            for h in range(2):
+                returned(g, h)
+
+
+def run_line(listed, q, kv, residual, router_t, idt, wgu, wdn, experts, cap, n_branch, n_seq):
+    rows, width = q.shape
     ff = wdn.shape[0]
     part = width // PARTS
+    tall = 2 * rows
+    steps = width // HEAD_SIZE * rows // tall // CHUNKS
     dma = pltpu.SemaphoreType.DMA
     return pl.pallas_call(
-        functools.partial(relay_kernel, cap, n_seq),
+        functools.partial(line_kernel, experts, cap, n_branch, n_seq),
         out_shape=jax.ShapeDtypeStruct((rows, width), BF16),
-        in_specs=[ANY, VMEM, VMEM, ANY, VMEM, ANY, ANY],
+        in_specs=[SMEM] + [VMEM] * 5 + [ANY, ANY],
         out_specs=VMEM,
         scratch_shapes=[
-            pltpu.VMEM((8 * cap, width), BF16),
-            pltpu.VMEM((8 * cap, width), BF16),
-            pltpu.VMEM((4 * cap, width), BF16),
+            pltpu.VMEM((n_seq, rows, kv.shape[1]), BF16),
+            pltpu.VMEM((n_branch - 1, rows, kv.shape[1]), BF16),
+            pltpu.VMEM((n_branch - 1, rows, kv.shape[1]), BF16),
+            pltpu.VMEM((CHUNKS, steps, tall, 1), F32),
+            pltpu.VMEM((CHUNKS, steps, tall, 1), F32),
+            pltpu.VMEM((rows, width), F32),
+            pltpu.VMEM((rows, width), BF16),
+            pltpu.VMEM((3, rows, width), BF16),
+            pltpu.VMEM((8, rows), F32),
+            pltpu.VMEM((3, 8, rows), F32),
+            pltpu.VMEM((4, 2, cap, width), BF16),
+            pltpu.VMEM((4, 2, cap, width), BF16),
+            pltpu.VMEM((4, 3, cap, width), BF16),
+            pltpu.VMEM((4, 3, cap, width), BF16),
             pltpu.VMEM((2, 2, width, ff), BF16),
             pltpu.VMEM((2, ff, width), BF16),
-            pltpu.VMEM((rows, width), F32),
+            pltpu.VMEM((3, PARTS, rows, part), BF16),
             pltpu.VMEM((2, PARTS, rows, part), BF16),
-            pltpu.VMEM((2, 8, rows), F32),
-            pltpu.VMEM((2, 4, cap, width), BF16),
-            pltpu.VMEM((2, 4, cap, width), BF16),
-            pltpu.VMEM((2, PARTS, rows, part), BF16),
-            pltpu.VMEM((PARTS, rows, part), BF16),
-            dma((2,)), dma((2,)), dma((2,)), dma,
-            dma((8,)), dma((8,)), dma((8,)), dma((8,)),
-            dma((PARTS,)), dma((2, PARTS)), dma, dma((2,)), dma((2, 4)),
-            dma((2, 4, PARTS)), dma((2, 4, PARTS)), dma((2, PARTS)), dma((PARTS,)),
+            dma, dma((n_seq - 1,)), dma((n_seq - 1,)), dma((n_branch - 1,)), dma((n_branch - 1,)),
+            dma((2,)), dma((2,)), dma((2,)),
+            dma((CHUNKS,)), dma((2, CHUNKS)), dma((PARTS,)), dma((PARTS,)), dma((2,)), dma((3,)),
+            dma((4, 3)), dma((4, 2)), dma((4, 2)), dma((4, 3, PARTS)), dma((3, PARTS)), dma((2, PARTS)),
         ],
         compiler_params=pltpu.CompilerParams(
             collective_id=2, has_side_effects=True, vmem_limit_bytes=VMEM_LIMIT
         ),
-    )(send, state, gate, normed, meta, wgu, wdn)
+    )(listed, q, kv, residual, router_t, idt, wgu, wdn)
 
 
 def on_device(
@@ -659,20 +862,21 @@
     capacity = 2 * ((3 * rows * top_count + 4 * experts - 1) // (4 * experts))
     cap = (capacity + 15) // 16 * 16
     kv = keyvals.reshape(rows, -1)
+    wgu = jnp.swapaxes(w_gate_up[0], 0, 1)
+    if n_branch == 4 and n_seq == 4 and experts == 8 and top_count == 2:
+        return run_line(
+            read_list.reshape(-1), queries[0], kv, residual[0], router.T, expert_ids[0].T,
+            wgu, w_down[0], experts, cap, n_branch, n_seq,
+        )[None]
     shifts = [
         lax.ppermute(kv, "seq", [(i, (i + step) % n_seq) for i in range(n_seq)])
         for step in range(1, n_seq)
     ]
     own = jnp.stack([kv] + shifts)
-    wgu = jnp.swapaxes(w_gate_up[0], 0, 1)
-    line = n_branch == 4 and n_seq == 4 and experts == 8 and top_count == 2
-    near = 4 if line else experts
     send, state, gate, normed, meta = attend(
         read_list.reshape(-1), queries[0], own, residual[0], router.T, expert_ids[0],
-        experts, near, cap, n_branch, n_seq,
+        experts, experts, cap, n_branch, n_seq,
     )
-    if line:
-        return run_relayed(send, state, gate, normed, meta, wgu, w_down[0], cap, n_seq)[None]
     return run_experts(send, state, gate, wgu, w_down[0], experts, cap, n_seq)[None]
 
 

time: 188 us -> 178 us (0.947)
  Pallas kernels: 172 us -> 168 us
  starting transfers between devices: 3.25 us -> 0 us
    pallas_call x2 -> x1, Pallas kernels: 172 us -> 168 us  [run_line(): pl.pallas_call(functools.partial(line_kernel, experts, cap, n_branch, n_s...]
    ppermute x3 -> x0, starting transfers between devices: 3.25 us -> none  [on_device(): lax.ppermute(kv, 'seq', [(i, (i + step) % n_seq) for i in range(n_seq)])]
  transfers between devices with their start and end apart: 3 -> 0, of which waited for: 0 -> 0; matrix products, arithmetic and copies ran while one was open for 5% -> 0% of each run, Pallas kernels for 0% -> 0%
where the time goes in v1:
time: 178 us
  Pallas kernels  168 us (94%)
  local copies, waits for them, and re-layouts  10.1 us (6%)
    pallas_call x1, Pallas kernels, run_line(): pl.pallas_call(functools.partial(line_kernel, experts, cap, n_branch, n_s...  168 us
    unnamed x3, local copies, waits for them, and re-layouts  10.1 us

profile of v1, /device:TPU:0, one launch (start us, length us, event | category | flops | bytes accessed | tf_op | source)
XLA Modules:
  0.0 178.1 jit_solution(16859084039869061998)
XLA Ops:
  0.0 1.6 copy.10
  1.6 6.2 %copy.12 = bf16[1,4096,2,384]{3,1,2,0:T(8,128)(2,1)} copy(bf16[1,4096,2,384]{3,2,1,0:T(2,128)(2,1)} %param.14) | data formatting | bytes 12582912 | tf_op args[6]
  7.8 168.0 %shard_map.82 = bf16[128,4096]{1,0:T(8,128)(2,1)} custom-call(s32[3]{0:T(128)} %bitcast.26, bf16[128,4096]{1,0:T(8,128)(2,1)} %bitcast.20, bf16[128,512]{1,0:T(8,128)(2,1)} %bitcast.22, bf16[128,4096]{1,0:T(8,128)(2,1)} %bitcast.21, bf16[8,4096]{1,0:T(8,128)(2,1)} %bitcast.24, s32[2,128]{1,0:T(2,128)} %bitcast.25, bf16[2,4096,384]{2,1,0:T(8,128)(2,1)} %bitcast.17, ...), custom_call_target="tpu_custom_call" | custom-call | tf_op jit(solution)/shard_map/pallas_call | solution.py:821
  175.8 2.3 %copy.14 = bf16[1,128,4096]{2,1,0:T(8,128)(2,1)} copy(bf16[1,128,4096]{2,1,0:T(8,128)(2,1)} %bitcast.18) | data formatting | bytes 2097152

commit v2 on v1

--- a/solution.py
+++ b/solution.py
@@ -9,9 +9,11 @@
 from jax.sharding import PartitionSpec as P
 
 HEAD_SIZE = 128
-PARTS = 4
+PARTS = 8
 CHUNKS = 4
+SLABS = 4
 VMEM_LIMIT = 60 * 1024 * 1024
+LINE_VMEM_LIMIT = 63 * 1024 * 1024
 F32 = jnp.float32
 BF16 = jnp.bfloat16
 ANY = pl.BlockSpec(memory_space=pl.ANY)
@@ -380,10 +382,10 @@
     list_ref, q_ref, kv_ref, res_ref, router_ref, idt_ref, wgu_ref, wdn_ref,
     out_ref,
     own, picked, sib, tops, totals, state, norm, raw, meta, xmeta,
-    recv, res, back, fwd, wgu, wdn, xout, fin,
-    kloc, ksend, krecv, ssend, srecv, wsend, wrecv, wloc,
+    recv, res, back, fwd, wraw, wgu, wdn, xout, fin,
+    ksend, krecv, ssend, srecv, wsend, wrecv, wloc,
     rowsend, rowrecv, relsend, relrecv, msend, mrecv,
-    fsend, drecv, bsend, brecv, osend, orecv,
+    fsend, drecv, bsend, brecv, lsend, osend, orecv,
 ):
     branch = lax.axis_index("branch")
     seq = lax.axis_index("seq")
@@ -423,12 +425,22 @@
         return slice(c * step, (c + 1) * step)
 
     twin = {"seq": seq + 1 - 2 * (seq % 2)}
-    weights = []
-    for i, (src, dst) in enumerate(((wgu_ref, wgu), (wdn_ref, wdn))):
-        weights.append(pltpu.make_async_copy(src, dst.at[0], wloc.at[i]))
-        weights.append(remote(src, dst.at[1], wsend.at[i], wrecv.at[i], twin))
-    mine = pltpu.make_async_copy(kv_ref, own.at[0], kloc)
-    mine.start()
+    slab = width // SLABS
+
+    def slab_in(i):
+        at = slice(i * slab, (i + 1) * slab)
+        return pltpu.make_async_copy(wgu_ref.at[at], wraw.at[at], wloc.at[i])
+
+    def slab_out(i):
+        at = slice(i * slab, (i + 1) * slab)
+        return remote(wgu.at[0, :, at], wgu.at[1, :, at], wsend.at[i], wrecv.at[i], twin)
+
+    down_in = pltpu.make_async_copy(wdn_ref, wdn.at[0], wloc.at[SLABS])
+    down_out = remote(wdn_ref, wdn.at[1], wsend.at[SLABS], wrecv.at[SLABS], twin)
+    for i in range(SLABS):
+        slab_in(i).start()
+    down_in.start()
+    own[0] = kv_ref[...].reshape(rows, own.shape[2])
 
     barrier = pltpu.get_barrier_semaphore()
     for shift in range(1, n_branch):
@@ -443,14 +455,22 @@
 
     def share(shift):
         return remote(
-            kv_ref, own.at[shift], ksend.at[shift - 1], krecv.at[shift - 1],
+            own.at[0], own.at[shift], ksend.at[shift - 1], krecv.at[shift - 1],
             {"seq": (seq + shift) % n_seq},
         )
 
     for shift in range(1, n_seq):
         share(shift).start()
-    for copy in weights:
-        copy.start()
+    down_out.start()
+    for i in range(SLABS):
+        slab_in(i).wait()
+
+        @pl.loop(0, slab // 256)
+        def _(j):
+            at = pl.ds(pl.multiple_of(i * slab + j * 256, 256), 256)
+            wgu[0, :, at] = jnp.swapaxes(wraw[at], 0, 1)
+
+        slab_out(i).start()
 
     idt = idt_ref[...]
     top_count = idt.shape[0]
@@ -466,7 +486,6 @@
         slot_t = jnp.sum(before_t * hot_t[k], axis=0, keepdims=True)
         meta[k : k + 1, :] = idt[k : k + 1, :].astype(F32) * float(cap) + slot_t
 
-    mine.wait()
     for shift in range(1, n_seq):
         share(shift).wait_recv()
     for offset in range(n_branch - 1):
@@ -633,22 +652,29 @@
     def whole(g, h):
         return remote(recv.at[g, h], recv.at[g, h], fsend.at[0, 0], drecv.at[g, h], places[1])
 
-    def home(g, f, c):
-        if f == 1:
-            return g, 0
-        return (0 if g == 1 else g), f - 1
-
-    def hand(g, f, c):
-        tg, slot = home(g, f, c)
-        h = 1 if f == 1 else f - 2
+    def back_to(g, c):
         return remote(
-            res.at[g, h, :, part(c)], back.at[tg, slot, :, part(c)],
-            bsend.at[g, h], brecv.at[tg, slot, c], places[f],
-        )
-
-    def compute(g):
+            res.at[g, 1, :, part(c)], back.at[g, 0, :, part(c)],
+            bsend.at[g, 1], brecv.at[g, 0, c], places[1],
+        )
+
+    def down_line(g, c):
+        slot = g // 2 * g
+        return remote(
+            res.at[g, 0, :, part(c)], back.at[slot, 1, :, part(c)],
+            bsend.at[g, 0], brecv.at[slot, 1, c], places[2],
+        )
+
+    def pass_on(g, c):
+        slot = g // 2 * g
+        return remote(
+            back.at[g, 0, :, part(c)], back.at[slot, 2, :, part(c)],
+            lsend.at[g - 1], brecv.at[slot, 2, c], places[2],
+        )
+
+    def compute(g, first=False):
         whole(g, 1).wait_recv()
-        if g:
+        if not first:
             pl.when(inner == 0)(lambda: whole(g, 0).wait_recv())
         x = recv[g].reshape(2 * cap, width)
         acts = []
@@ -660,19 +686,17 @@
             done = jnp.dot(acts[0], wdn[0, :, part(c)], preferred_element_type=F32)
             done += jnp.dot(acts[1], wdn[1, :, part(c)], preferred_element_type=F32)
             res[g, :, :, part(c)] = done.astype(BF16).reshape(2, cap, step)
-            if g == 0:
-                hand(0, 1, c).start()
-            else:
-
-                def side():
-                    hand(g, 1, c).start()
-
-                def up_line():
-                    hand(g, 3, c).start()
-                    hand(g, 2, c).start()
-
-                pl.when(inner == 1)(side)
-                pl.when(inner == 0)(up_line)
+            back_to(g, c).start()
+
+    def pass_all(g):
+        if g == 1:
+            for c in range(PARTS):
+                down_line(g, c).start()
+        for c in range(PARTS):
+            back_to(g, c).wait_recv()
+            if g > 1:
+                down_line(g, c).start()
+            pass_on(g, c).start()
 
     def combined(g, count, weight, c):
         for f in range(count - 1):
@@ -707,65 +731,64 @@
     is_inner(lambda: give_all(0, 4))
     is_outer(lambda: give_all(0, 2))
 
-    for copy in weights:
-        copy.wait()
-    compute(0)
+    for i in range(SLABS):
+        slab_out(i).wait_recv()
+    down_out.wait_recv()
+    down_in.wait()
+
+    is_inner(lambda: compute(0, True))
+
+    def far_rows(c, pick):
+        remote(
+            raw.at[2, :, part(c)], raw.at[2, :, part(c)], relsend.at[0], relrecv.at[c], places[2]
+        ).wait_recv()
+        give(3, 4, pick, c)
 
     @is_inner
     def _():
         wait_rows(1)
+        meta_relay().start()
         for c in range(PARTS):
             relay(c).start()
-        meta_relay().start()
         wait_rows(2)
         give_all(2, 4)
-        give_all(1, 2)
-
-    compute(1)
-
-    def far_rows(c):
-        relay_in = remote(
-            raw.at[2, :, part(c)], raw.at[2, :, part(c)], relsend.at[0], relrecv.at[c], places[2]
-        )
-        relay_in.wait_recv()
+        wait_rows(3)
+        far_rows(0, picks(3, 4))
+
+    compute(1 + inner)
+    is_outer(lambda: pass_all(1))
+
+    def send_far(s, span):
+        weight = shares(2 + s, 4)
+        for c in span:
+            xout[s, c] = combined(2 + s, 4, weight, c).astype(BF16)
+            result(s, c).start()
+
+    def settle(count):
+        weight = shares(0, count)
+        for c in range(PARTS):
+            state[:, part(c)] += combined(0, count, weight, c)
 
     @is_inner
     def _():
-        wait_rows(3)
         pick = picks(3, 4)
-        for c in range(PARTS):
-            far_rows(c)
-            give(3, 4, pick, c)
-
-    compute(2)
-    compute(3)
+        for c in range(1, PARTS):
+            far_rows(c, pick)
+        give_all(1, 2)
+        send_far(0, range(PARTS // 2))
+
+    compute(2 + inner)
+    is_inner(lambda: send_far(0, range(PARTS // 2, PARTS)))
+    is_outer(lambda: pass_all(2))
+    compute(3 - 2 * inner)
+
+    def arrived(s, c):
+        remote(fin.at[s, c], fin.at[s, c], osend.at[0, 0], orecv.at[s, c], places[2]).wait_recv()
 
     @is_inner
     def _():
-        for s in range(2):
-            weight = shares(2 + s, 4)
-            for c in range(PARTS):
-                xout[s, c] = combined(2 + s, 4, weight, c).astype(BF16)
-                result(s, c).start()
-        weight = shares(0, 4)
-        for c in range(PARTS):
-            state[:, part(c)] += combined(0, 4, weight, c)
-
-    @is_outer
-    def _():
-        weight = shares(0, 2)
-        for c in range(PARTS):
-            state[:, part(c)] += combined(0, 2, weight, c)
-
-    def arrived(s, c):
-        remote(fin.at[s, c], fin.at[s, c], osend.at[0, 0], orecv.at[s, c], places[2]).wait_recv()
-
-    for c in range(PARTS):
-        arrived(0, c)
-        out_ref[:, part(c)] = (state[:, part(c)] + fin[0, c].astype(F32)).astype(BF16)
-
-    @is_inner
-    def _():
+        settle(4)
+        send_far(1, range(PARTS))
         weight = shares(1, 2)
         for c in range(PARTS):
             partial = combined(1, 2, weight, c)
@@ -773,8 +796,21 @@
             xout[2, c] = (partial + fin[1, c].astype(F32)).astype(BF16)
             result(2, c).start()
 
+    @is_outer
+    def _():
+        pass_all(3)
+        compute(0, True)
+        settle(2)
+
+    for c in range(PARTS):
+        arrived(0, c)
+        out_ref[:, part(c)] = (state[:, part(c)] + fin[0, c].astype(F32)).astype(BF16)
+
     for shift in range(1, n_seq):
         share(shift).wait_send()
+    for i in range(SLABS):
+        slab_out(i).wait_send()
+    down_out.wait_send()
     for offset in range(n_branch - 1):
         lend(offset).wait_send()
     for r in range(CHUNKS):
@@ -788,7 +824,8 @@
         remote(res.at[g, h], res.at[g, h], bsend.at[g, h], brecv.at[0, 0, 0], places[1]).wait_send()
 
     sent(0, 1)
-    returned(0, 1)
+    for g in range(4):
+        returned(g, 1)
 
     @is_inner
     def _():
@@ -796,8 +833,6 @@
             for f in ((2, 3) if g == 0 else (1, 2, 3)):
                 sent(g, f)
         sent(1, 1)
-        for g in (1, 2, 3):
-            returned(g, 1)
         for c in range(PARTS):
             relay(c).wait_send()
             for s in range(3):
@@ -807,13 +842,14 @@
     @is_outer
     def _():
         for g in (1, 2, 3):
-            for h in range(2):
-                returned(g, h)
+            returned(g, 0)
+            remote(back.at[g, 0], back.at[g, 0], lsend.at[g - 1], brecv.at[0, 0, 0], places[2]).wait_send()
 
 
 def run_line(listed, q, kv, residual, router_t, idt, wgu, wdn, experts, cap, n_branch, n_seq):
     rows, width = q.shape
     ff = wdn.shape[0]
+    kv_width = kv.shape[1] * kv.shape[2]
     part = width // PARTS
     tall = 2 * rows
     steps = width // HEAD_SIZE * rows // tall // CHUNKS
@@ -824,9 +860,9 @@
         in_specs=[SMEM] + [VMEM] * 5 + [ANY, ANY],
         out_specs=VMEM,
         scratch_shapes=[
-            pltpu.VMEM((n_seq, rows, kv.shape[1]), BF16),
-            pltpu.VMEM((n_branch - 1, rows, kv.shape[1]), BF16),
-            pltpu.VMEM((n_branch - 1, rows, kv.shape[1]), BF16),
+            pltpu.VMEM((n_seq, rows, kv_width), BF16),
+            pltpu.VMEM((n_branch - 1, rows, kv_width), BF16),
+            pltpu.VMEM((n_branch - 1, rows, kv_width), BF16),
             pltpu.VMEM((CHUNKS, steps, tall, 1), F32),
             pltpu.VMEM((CHUNKS, steps, tall, 1), F32),
             pltpu.VMEM((rows, width), F32),
@@ -838,17 +874,18 @@
             pltpu.VMEM((4, 2, cap, width), BF16),
             pltpu.VMEM((4, 3, cap, width), BF16),
             pltpu.VMEM((4, 3, cap, width), BF16),
+            pltpu.VMEM((width, 2, ff), BF16),
             pltpu.VMEM((2, 2, width, ff), BF16),
             pltpu.VMEM((2, ff, width), BF16),
             pltpu.VMEM((3, PARTS, rows, part), BF16),
             pltpu.VMEM((2, PARTS, rows, part), BF16),
-            dma, dma((n_seq - 1,)), dma((n_seq - 1,)), dma((n_branch - 1,)), dma((n_branch - 1,)),
-            dma((2,)), dma((2,)), dma((2,)),
+            dma((n_seq - 1,)), dma((n_seq - 1,)), dma((n_branch - 1,)), dma((n_branch - 1,)),
+            dma((SLABS + 1,)), dma((SLABS + 1,)), dma((SLABS + 1,)),
             dma((CHUNKS,)), dma((2, CHUNKS)), dma((PARTS,)), dma((PARTS,)), dma((2,)), dma((3,)),
-            dma((4, 3)), dma((4, 2)), dma((4, 2)), dma((4, 3, PARTS)), dma((3, PARTS)), dma((2, PARTS)),
+            dma((4, 3)), dma((4, 2)), dma((4, 2)), dma((4, 3, PARTS)), dma((3,)), dma((3, PARTS)), dma((2, PARTS)),
         ],
         compiler_params=pltpu.CompilerParams(
-            collective_id=2, has_side_effects=True, vmem_limit_bytes=VMEM_LIMIT
+            collective_id=2, has_side_effects=True, vmem_limit_bytes=LINE_VMEM_LIMIT
         ),
     )(listed, q, kv, residual, router_t, idt, wgu, wdn)
 
@@ -861,13 +898,13 @@
     top_count = expert_ids.shape[2]
     capacity = 2 * ((3 * rows * top_count + 4 * experts - 1) // (4 * experts))
     cap = (capacity + 15) // 16 * 16
+    if n_branch == 4 and n_seq == 4 and experts == 8 and top_count == 2:
+        return run_line(
+            read_list.reshape(-1), queries[0], keyvals[0], residual[0], router.T, expert_ids[0].T,
+            w_gate_up[0], w_down[0], experts, cap, n_branch, n_seq,
+        )[None]
     kv = keyvals.reshape(rows, -1)
     wgu = jnp.swapaxes(w_gate_up[0], 0, 1)
-    if n_branch == 4 and n_seq == 4 and experts == 8 and top_count == 2:
-        return run_line(
-            read_list.reshape(-1), queries[0], kv, residual[0], router.T, expert_ids[0].T,
-            wgu, w_down[0], experts, cap, n_branch, n_seq,
-        )[None]
     shifts = [
         lax.ppermute(kv, "seq", [(i, (i + step) % n_seq) for i in range(n_seq)])
         for step in range(1, n_seq)

time: 178 us -> 143 us (0.80)
  Pallas kernels: 168 us -> 140 us
  local copies, waits for them, and re-layouts: 10.1 us -> 2.29 us
    pallas_call x1, Pallas kernels: 168 us -> 140 us  [run_line(): pl.pallas_call(functools.partial(line_kernel, experts, cap, n_branch, n_s...]
    unnamed x3 -> x1, local copies, waits for them, and re-layouts: 10.1 us -> 2.29 us
where the time goes in v2:
time: 143 us
  Pallas kernels  140 us (98%)
  local copies, waits for them, and re-layouts  2.29 us (2%)
    pallas_call x1, Pallas kernels, run_line(): pl.pallas_call(functools.partial(line_kernel, experts, cap, n_branch, n_s...  140 us

profile of v2, /device:TPU:0, one launch (start us, length us, event | category | flops | bytes accessed | tf_op | source)
XLA Modules:
  0.0 142.6 jit_solution(5384241250815751264)
XLA Ops:
  0.0 140.3 %shard_map.82 = bf16[128,4096]{1,0:T(8,128)(2,1)} custom-call(s32[3]{0:T(128)} %bitcast.19, bf16[128,4096]{1,0:T(8,128)(2,1)} %bitcast.14, bf16[128,2,256]{2,1,0:T(2,128)(2,1)} %bitcast.16, bf16[128,4096]{1,0:T(8,128)(2,1)} %bitcast.15, bf16[8,4096]{1,0:T(8,128)(2,1)} %bitcast.17, s32[2,128]{1,0:T(2,128)} %bitcast.18, bf16[4096,2,384]{2,1,0:T(2,128)(2,1)} %bitcast.11, ...), custom_call_target="tpu_custom_call" | custom-call | tf_op jit(solution)/shard_map/pallas_call | solution.py:857
  140.3 2.3 %copy.10 = bf16[1,128,4096]{2,1,0:T(8,128)(2,1)} copy(bf16[1,128,4096]{2,1,0:T(8,128)(2,1)} %bitcast.12) | data formatting | bytes 2097152

commit v3 on v2

--- a/solution.py
+++ b/solution.py
@@ -10,7 +10,7 @@
 
 HEAD_SIZE = 128
 PARTS = 8
-CHUNKS = 4
+CHUNKS = 8
 SLABS = 4
 VMEM_LIMIT = 60 * 1024 * 1024
 LINE_VMEM_LIMIT = 63 * 1024 * 1024
@@ -382,10 +382,10 @@
     list_ref, q_ref, kv_ref, res_ref, router_ref, idt_ref, wgu_ref, wdn_ref,
     out_ref,
     own, picked, sib, tops, totals, state, norm, raw, meta, xmeta,
-    recv, res, back, fwd, wraw, wgu, wdn, xout, fin,
+    recv, res, back, fwd, wraw, wgu, wdn, xout, fin, done,
     ksend, krecv, ssend, srecv, wsend, wrecv, wloc,
     rowsend, rowrecv, relsend, relrecv, msend, mrecv,
-    fsend, drecv, bsend, brecv, lsend, osend, orecv,
+    fsend, drecv, bsend, brecv, lsend, osend, orecv, dsend,
 ):
     branch = lax.axis_index("branch")
     seq = lax.axis_index("seq")
@@ -488,8 +488,6 @@
 
     for shift in range(1, n_seq):
         share(shift).wait_recv()
-    for offset in range(n_branch - 1):
-        picked[offset] = own[(seq - list_ref[offset] + n_seq) % n_seq]
 
     def lend(offset):
         return remote(
@@ -497,7 +495,10 @@
             {"branch": (branch + offset + 1) % n_branch},
         )
 
-    for offset in range(n_branch - 1):
+    upper = branch // 2
+    for target in (2 - upper, near, 3 - 3 * upper):
+        offset = (target - branch + n_branch - 1) % n_branch
+        picked[offset] = own[(seq - list_ref[offset] + n_seq) % n_seq]
         lend(offset).start()
 
     def chunk(r):
@@ -589,9 +590,20 @@
 
     meta_out().start()
 
+    early = CHUNKS // 2
+    late = slice(early * span, rows)
+
     def relay(c):
         return remote(
-            raw.at[0, :, part(c)], raw.at[2, :, part(c)], relsend.at[c], relrecv.at[c], {"branch": far}
+            raw.at[0, late, part(c)], raw.at[2, late, part(c)], relsend.at[c], relrecv.at[c],
+            {"branch": far},
+        )
+
+    def relay_rows(r):
+        at = slice(r * span, (r + 1) * span)
+        return remote(
+            raw.at[0, at], raw.at[2, at], relsend.at[PARTS + r], relrecv.at[PARTS + r],
+            {"branch": far},
         )
 
     def meta_relay():
@@ -641,8 +653,9 @@
         recv[g, 0, :, part(c)] = taken[:cap]
         for f in range(1, count):
             fwd[g, f - 1, :, part(c)] = taken[f * cap : (f + 1) * cap]
-        for f in ((3, 2, 1) if count == 4 else (1,)):
-            forward(g, f, c).start()
+        for f in (3, 2, 1):
+            if f < count and (g, f) != (2, 2):
+                forward(g, f, c).start()
 
     def give_all(g, count):
         pick = picks(g, count)
@@ -672,7 +685,7 @@
             lsend.at[g - 1], brecv.at[slot, 2, c], places[2],
         )
 
-    def compute(g, first=False):
+    def compute(g, first=False, quiet=False):
         whole(g, 1).wait_recv()
         if not first:
             pl.when(inner == 0)(lambda: whole(g, 0).wait_recv())
@@ -683,20 +696,44 @@
             up = jnp.dot(x, wgu[h, 1], preferred_element_type=F32)
             acts.append((gate / (1.0 + jnp.exp(-gate)) * up).astype(BF16))
         for c in range(PARTS):
-            done = jnp.dot(acts[0], wdn[0, :, part(c)], preferred_element_type=F32)
-            done += jnp.dot(acts[1], wdn[1, :, part(c)], preferred_element_type=F32)
-            res[g, :, :, part(c)] = done.astype(BF16).reshape(2, cap, step)
-            back_to(g, c).start()
-
-    def pass_all(g):
-        if g == 1:
-            for c in range(PARTS):
-                down_line(g, c).start()
+            total = jnp.dot(acts[0], wdn[0, :, part(c)], preferred_element_type=F32)
+            total += jnp.dot(acts[1], wdn[1, :, part(c)], preferred_element_type=F32)
+            res[g, :, :, part(c)] = total.astype(BF16).reshape(2, cap, step)
+            if not quiet:
+                back_to(g, c).start()
+
+    def compute_half(g, h, opening):
+        if opening:
+            pl.when(inner == 0)(lambda: whole(g, h).wait_recv())
+        else:
+            whole(g, h).wait_recv()
+        x = recv[g, h]
+        acts = []
+        for i in range(2):
+            gate = jnp.dot(x, wgu[i, 0], preferred_element_type=F32)
+            up = jnp.dot(x, wgu[i, 1], preferred_element_type=F32)
+            acts.append((gate / (1.0 + jnp.exp(-gate)) * up).astype(BF16))
         for c in range(PARTS):
-            back_to(g, c).wait_recv()
-            if g > 1:
-                down_line(g, c).start()
-            pass_on(g, c).start()
+            total = jnp.dot(acts[0], wdn[0, :, part(c)], preferred_element_type=F32)
+            total += jnp.dot(acts[1], wdn[1, :, part(c)], preferred_element_type=F32)
+            res[g, h, :, part(c)] = total.astype(BF16)
+            pl.when(inner == 1 - opening)(lambda: back_to(g, c).start())
+            if not opening and c < PARTS // 2:
+                pl.when(inner == 0)(lambda: down_line(g, c).start())
+
+    def start_all(copy, g):
+        for c in range(PARTS):
+            copy(g, c).start()
+
+    def pass_part(g, c):
+        back_to(g, c).wait_recv()
+        pass_on(g, c).start()
+
+    def pass_all(g, first, ahead):
+        for c in range(first, PARTS):
+            pass_part(g, c)
+            if ahead and c - first + ahead < PARTS:
+                down_line(g, c - first + ahead).start()
 
     def combined(g, count, weight, c):
         for f in range(count - 1):
@@ -716,14 +753,15 @@
             return remote(xout.at[2, c], fin.at[0, c], osend.at[2, c], orecv.at[0, c], {"branch": near})
         return remote(xout.at[s, c], fin.at[s, c], osend.at[s, c], orecv.at[s, c], {"branch": far})
 
-    def wait_rows(g):
+    def wait_meta(g):
         remote(xmeta.at[g - 1], xmeta.at[g - 1], msend.at[0], mrecv.at[g - 1], places[2]).wait_recv()
-        if g < 3:
-            for r in range(CHUNKS):
-                at = slice(r * span, (r + 1) * span)
-                remote(
-                    raw.at[g - 1, at], raw.at[g - 1, at], rowsend.at[0], rowrecv.at[g - 1, r], places[2]
-                ).wait_recv()
+
+    def wait_chunks(g, chunks):
+        for r in chunks:
+            at = slice(r * span, (r + 1) * span)
+            remote(
+                raw.at[g - 1, at], raw.at[g - 1, at], rowsend.at[0], rowrecv.at[g - 1, r], places[2]
+            ).wait_recv()
 
     is_inner = pl.when(inner == 1)
     is_outer = pl.when(inner == 0)
@@ -736,33 +774,39 @@
     down_out.wait_recv()
     down_in.wait()
 
-    is_inner(lambda: compute(0, True))
 
     def far_rows(c, pick):
-        remote(
-            raw.at[2, :, part(c)], raw.at[2, :, part(c)], relsend.at[0], relrecv.at[c], places[2]
-        ).wait_recv()
+        relay(c).wait_recv()
         give(3, 4, pick, c)
 
     @is_inner
     def _():
-        wait_rows(1)
+        wait_chunks(1, range(early))
+        for r in range(early):
+            relay_rows(r).start()
+        compute(0, True)
+        wait_chunks(1, range(early, CHUNKS))
+        wait_meta(1)
         meta_relay().start()
         for c in range(PARTS):
             relay(c).start()
-        wait_rows(2)
+        wait_chunks(2, range(CHUNKS))
+        wait_meta(2)
         give_all(2, 4)
-        wait_rows(3)
+        for c in range(PARTS):
+            forward(2, 2, c).start()
+        wait_meta(3)
+        for r in range(early):
+            relay_rows(r).wait_recv()
         far_rows(0, picks(3, 4))
 
-    compute(1 + inner)
-    is_outer(lambda: pass_all(1))
-
-    def send_far(s, span):
-        weight = shares(2 + s, 4)
-        for c in span:
-            xout[s, c] = combined(2 + s, 4, weight, c).astype(BF16)
-            result(s, c).start()
+    compute(1 + inner, quiet=True)
+    is_inner(lambda: start_all(back_to, 2))
+    is_outer(lambda: start_all(down_line, 1))
+
+    def send_far(s, weight, c):
+        xout[s, c] = combined(2 + s, 4, weight, c).astype(BF16)
+        result(s, c).start()
 
     def settle(count):
         weight = shares(0, count)
@@ -775,37 +819,74 @@
         for c in range(1, PARTS):
             far_rows(c, pick)
         give_all(1, 2)
-        send_far(0, range(PARTS // 2))
-
-    compute(2 + inner)
-    is_inner(lambda: send_far(0, range(PARTS // 2, PARTS)))
-    is_outer(lambda: pass_all(2))
+
+    lead = PARTS // 4
+    compute_half(2 + inner, 1 - inner, 1)
+
+    @is_outer
+    def _():
+        for c in range(lead):
+            pass_part(2, c)
+
+    @is_inner
+    def _():
+        weight = shares(2, 4)
+        for c in range(PARTS // 2):
+            send_far(0, weight, c)
+
+    compute_half(2 + inner, inner, 0)
+    is_outer(lambda: pass_all(2, lead, 2 * lead))
+
+    @is_inner
+    def _():
+        weight = shares(2, 4)
+        for c in range(PARTS // 2, PARTS):
+            send_far(0, weight, c)
+
     compute(3 - 2 * inner)
 
     def arrived(s, c):
         remote(fin.at[s, c], fin.at[s, c], osend.at[0, 0], orecv.at[s, c], places[2]).wait_recv()
 
+    def send_near(weight, c):
+        partial = combined(1, 2, weight, c)
+        arrived(1, c)
+        xout[2, c] = (partial + fin[1, c].astype(F32)).astype(BF16)
+        result(2, c).start()
+
     @is_inner
     def _():
+        near_weight = shares(1, 2)
+        weight = shares(3, 4)
+        lag = PARTS // 2
+        for c in range(PARTS):
+            send_far(1, weight, c)
+            if c >= lag:
+                send_near(near_weight, c - lag)
+        for c in range(PARTS - lag, PARTS):
+            send_near(near_weight, c)
         settle(4)
-        send_far(1, range(PARTS))
-        weight = shares(1, 2)
-        for c in range(PARTS):
-            partial = combined(1, 2, weight, c)
-            arrived(1, c)
-            xout[2, c] = (partial + fin[1, c].astype(F32)).astype(BF16)
-            result(2, c).start()
 
     @is_outer
     def _():
-        pass_all(3)
+        for c in range(lead):
+            down_line(3, c).start()
+        pass_all(3, 0, lead)
+        start_all(back_to, 1)
         compute(0, True)
+        pass_all(1, 0, 0)
         settle(2)
+
+    def write(c):
+        return pltpu.make_async_copy(done.at[:, part(c)], out_ref.at[:, part(c)], dsend.at[c])
 
     for c in range(PARTS):
         arrived(0, c)
-        out_ref[:, part(c)] = (state[:, part(c)] + fin[0, c].astype(F32)).astype(BF16)
-
+        done[:, part(c)] = (state[:, part(c)] + fin[0, c].astype(F32)).astype(BF16)
+        write(c).start()
+
+    for c in range(PARTS):
+        write(c).wait()
     for shift in range(1, n_seq):
         share(shift).wait_send()
     for i in range(SLABS):
@@ -835,6 +916,8 @@
         sent(1, 1)
         for c in range(PARTS):
             relay(c).wait_send()
+            if c < early:
+                relay_rows(c).wait_send()
             for s in range(3):
                 result(s, c).wait_send()
         meta_relay().wait_send()
@@ -858,7 +941,7 @@
         functools.partial(line_kernel, experts, cap, n_branch, n_seq),
         out_shape=jax.ShapeDtypeStruct((rows, width), BF16),
         in_specs=[SMEM] + [VMEM] * 5 + [ANY, ANY],
-        out_specs=VMEM,
+        out_specs=ANY,
         scratch_shapes=[
             pltpu.VMEM((n_seq, rows, kv_width), BF16),
             pltpu.VMEM((n_branch - 1, rows, kv_width), BF16),
@@ -879,10 +962,11 @@
             pltpu.VMEM((2, ff, width), BF16),
             pltpu.VMEM((3, PARTS, rows, part), BF16),
             pltpu.VMEM((2, PARTS, rows, part), BF16),
+            pltpu.VMEM((rows, width), BF16),
             dma((n_seq - 1,)), dma((n_seq - 1,)), dma((n_branch - 1,)), dma((n_branch - 1,)),
             dma((SLABS + 1,)), dma((SLABS + 1,)), dma((SLABS + 1,)),
-            dma((CHUNKS,)), dma((2, CHUNKS)), dma((PARTS,)), dma((PARTS,)), dma((2,)), dma((3,)),
-            dma((4, 3)), dma((4, 2)), dma((4, 2)), dma((4, 3, PARTS)), dma((3,)), dma((3, PARTS)), dma((2, PARTS)),
+            dma((CHUNKS,)), dma((2, CHUNKS)), dma((PARTS + CHUNKS // 2,)), dma((PARTS + CHUNKS // 2,)), dma((2,)), dma((3,)),
+            dma((4, 3)), dma((4, 2)), dma((4, 2)), dma((4, 3, PARTS)), dma((3,)), dma((3, PARTS)), dma((2, PARTS)), dma((PARTS,)),
         ],
         compiler_params=pltpu.CompilerParams(
             collective_id=2, has_side_effects=True, vmem_limit_bytes=LINE_VMEM_LIMIT

time: 143 us -> 135 us (0.944)
  Pallas kernels: 140 us -> 133 us
    pallas_call x1, Pallas kernels: 140 us -> 133 us  [run_line(): pl.pallas_call(functools.partial(line_kernel, experts, cap, n_branch, n_s...]
where the time goes in v3:
time: 135 us
  Pallas kernels  133 us (99%)
  local copies, waits for them, and re-layouts  2.29 us (2%)
    pallas_call x1, Pallas kernels, run_line(): pl.pallas_call(functools.partial(line_kernel, experts, cap, n_branch, n_s...  133 us

profile of v3, /device:TPU:0, one launch (start us, length us, event | category | flops | bytes accessed | tf_op | source)
XLA Modules:
  0.0 135.1 jit_solution(15124159693062830226)
XLA Ops:
  0.0 132.8 %shard_map.82 = bf16[128,4096]{1,0:T(8,128)(2,1)} custom-call(s32[3]{0:T(128)} %bitcast.19, bf16[128,4096]{1,0:T(8,128)(2,1)} %bitcast.14, bf16[128,2,256]{2,1,0:T(2,128)(2,1)} %bitcast.16, bf16[128,4096]{1,0:T(8,128)(2,1)} %bitcast.15, bf16[8,4096]{1,0:T(8,128)(2,1)} %bitcast.17, s32[2,128]{1,0:T(2,128)} %bitcast.18, bf16[4096,2,384]{2,1,0:T(2,128)(2,1)} %bitcast.11, ...), custom_call_target="tpu_custom_call" | custom-call | tf_op jit(solution)/shard_map/pallas_call | solution.py:940
  132.8 2.3 %copy.10 = bf16[1,128,4096]{2,1,0:T(8,128)(2,1)} copy(bf16[1,128,4096]{2,1,0:T(8,128)(2,1)} %bitcast.12) | data formatting | bytes 2097152

commit v4 on v3

--- a/solution.py
+++ b/solution.py
@@ -785,16 +785,16 @@
         for r in range(early):
             relay_rows(r).start()
         compute(0, True)
+        wait_chunks(2, range(CHUNKS))
+        wait_meta(2)
+        give_all(2, 4)
+        for c in range(PARTS):
+            forward(2, 2, c).start()
         wait_chunks(1, range(early, CHUNKS))
         wait_meta(1)
         meta_relay().start()
         for c in range(PARTS):
             relay(c).start()
-        wait_chunks(2, range(CHUNKS))
-        wait_meta(2)
-        give_all(2, 4)
-        for c in range(PARTS):
-            forward(2, 2, c).start()
         wait_meta(3)
         for r in range(early):
             relay_rows(r).wait_recv()

time: 135 us -> 134 us (level)
  no operation moved by 1% of the time
where the time goes in v4:
time: 134 us
  Pallas kernels  132 us (99%)
  local copies, waits for them, and re-layouts  2.29 us (2%)
    pallas_call x1, Pallas kernels, run_line(): pl.pallas_call(functools.partial(line_kernel, experts, cap, n_branch, n_s...  132 us

profile of v4, /device:TPU:0, one launch (start us, length us, event | category | flops | bytes accessed | tf_op | source)
XLA Modules:
  0.0 134.2 jit_solution(14076935273979744140)
XLA Ops:
  0.0 131.9 %shard_map.82 = bf16[128,4096]{1,0:T(8,128)(2,1)} custom-call(s32[3]{0:T(128)} %bitcast.19, bf16[128,4096]{1,0:T(8,128)(2,1)} %bitcast.14, bf16[128,2,256]{2,1,0:T(2,128)(2,1)} %bitcast.16, bf16[128,4096]{1,0:T(8,128)(2,1)} %bitcast.15, bf16[8,4096]{1,0:T(8,128)(2,1)} %bitcast.17, s32[2,128]{1,0:T(2,128)} %bitcast.18, bf16[4096,2,384]{2,1,0:T(2,128)(2,1)} %bitcast.11, ...), custom_call_target="tpu_custom_call" | custom-call | tf_op jit(solution)/shard_map/pallas_call | solution.py:940
  131.9 2.3 %copy.10 = bf16[1,128,4096]{2,1,0:T(8,128)(2,1)} copy(bf16[1,128,4096]{2,1,0:T(8,128)(2,1)} %bitcast.12) | data formatting | bytes 2097152
